TPU v7x, 32 devices: a whole 2x2x4 slice. The times are simulated.
32 devices in a mesh: row: 4 (over y, x), col: 8 (over z, core).
Axes of the slice: x: 2, y: 2, z: 4, core: 2. Of those that a mesh axis runs over, the one named last changes fastest.
Arguments:
- inverse: float32 [24576, 24576], P('row', 'col'), may hold values from -0.0546875 to 0.0546875
- parent_panel: float32 [24576, 256], P(('row', 'col')), may hold values from -1.8 to 1.8
- child_panel: float32 [24576, 256], P(('row', 'col')), may hold values from -1.8 to 1.8
- child_top: float32 [256, 256], replicated, may hold values from -0.375 to 0.375
- diag_parent: float32 [256, 256], replicated, may hold values from -12 to 12
- diag_child: float32 [256, 256], replicated, may hold values from -12 to 12
- parent_blocks: int32 [192], replicated, may hold values from 0 to 1
- child_blocks: int32 [192], replicated, may hold values from 0 to 1, as said below
Outputs:
- parent_column: float32 [24576, 256], P(('row', 'col'))
- parent_diagonal: float32 [256, 256], replicated
- child_column: float32 [24576, 256], P(('row', 'col'))
- child_upper: float32 [256, 256], replicated
- child_diagonal: float32 [256, 256], replicated
Inputs may be any that keep to these rules, and one draw needn't show every extreme that they name: `child_blocks`: each entry is 0 or 1, and is 1 only where parent_blocks is 1.
All inputs are finite; a program needn't handle non-finite values.
Results may differ from a plain program's by a relative error of at most 0.000086.
Values sent between devices are 32-bit elements; how exact they have to be, the bound alone decides.
A program may use at most 192 MiB of HBM per device.

v0:
```python
import jax
import jax.numpy as jnp
from jax import lax
from jax.sharding import PartitionSpec as P

BLK = 128


HIGHEST = lax.Precision.HIGHEST


def spread(value, axis, source):
    kept = jnp.where(lax.axis_index(axis) == source, value, 0).astype(value.dtype)
    return lax.psum(kept, axis)


def matmul(left, right):
    return jnp.dot(left, right, precision=HIGHEST, preferred_element_type=jnp.float32)


def local_mask(blocks, rows_here):
    flags = jnp.repeat(blocks, BLK, total_repeat_length=blocks.shape[0] * BLK)
    device = lax.axis_index("row") * lax.axis_size("col") + lax.axis_index("col")
    local_flags = lax.dynamic_slice_in_dim(flags, device * rows_here, rows_here, 0)
    return local_flags.astype(jnp.float32)[:, None]


def column_slice(block_rows, tile_cols):
    col_ratio = lax.axis_size("col") // lax.axis_size("row")
    index_col = lax.axis_index("col")
    wanted = lax.dynamic_slice_in_dim(block_rows, index_col % col_ratio * tile_cols, tile_cols, 0)
    return (wanted, index_col // col_ratio)


def apply_inverse(inverse, panel):
    rows_here = panel.shape[0]
    block_rows = lax.all_gather(panel, "col", axis=0, tiled=True)
    wanted, owner_row = column_slice(block_rows, inverse.shape[1])
    column_rows = spread(wanted, "row", owner_row)
    return lax.psum_scatter(
        matmul(lax.slice_in_dim(inverse, 0, rows_here * lax.axis_size("col"), axis=0), column_rows),
        "col",
        scatter_dimension=0,
        tiled=True,
    )


def per_device(
    inverse,
    parent_panel,
    child_panel,
    child_top,
    diag_parent,
    diag_child,
    parent_blocks,
    child_blocks,
):
    rows_here = parent_panel.shape[0]
    parent_mask = local_mask(parent_blocks, rows_here)
    child_mask = local_mask(child_blocks, rows_here)
    parent_masked = parent_panel * parent_mask
    child_masked = child_panel * child_mask
    parent_image = apply_inverse(inverse, parent_masked)
    child_image = apply_inverse(inverse, child_masked)
    parent_column = -(parent_mask * parent_image)
    parent_local = matmul(parent_masked.T, parent_column)
    cross_local = matmul(parent_column.T, child_masked)
    carried = matmul(parent_column, child_top)
    child_column = -(child_mask * (carried + child_image))
    image_local = matmul(child_masked.T, child_image)
    parent_sum, cross_sum, image_sum = lax.psum(
        (parent_local, cross_local, image_local), ("row", "col")
    )
    parent_diagonal = diag_parent - parent_sum
    child_upper = -(matmul(parent_diagonal, child_top) + cross_sum)
    child_diagonal = (
        diag_child - matmul(child_top.T, child_upper) + matmul(cross_sum.T, child_top) + image_sum
    )
    return (parent_column, parent_diagonal, child_column, child_upper, child_diagonal)


def solution(mesh):
    placed = (
        P("row", "col"),
        P(("row", "col"), None),
        P(("row", "col"), None),
        P(),
        P(),
        P(),
        P(),
        P(),
    )
    return jax.shard_map(
        per_device,
        mesh=mesh,
        in_specs=placed,
        out_specs=(P(("row", "col"), None), P(), P(("row", "col"), None), P(), P()),
        check_vma=False,
    )
```

profile of v0, /device:TPU:0, one launch (start us, length us, event | category | flops | bytes accessed | tf_op | source)
XLA Modules:
  0.0 949.8 jit_solution(11591505820948566814)
XLA Ops:
  7.3 0.8 add_bitcast_fusion.1
  8.0 1.9 scatter_custom_fusion
  10.2 0.3 reduce-window.21
  11.1 151.8 %gather_fusion = s32[24576]{0:T(1024)S(1)} fusion(s32[192]{0:T(256)S(1)} %copy-done.1, s32[24576]{0:T(1024)S(1)} %fusion.5), kind=kCustom, calls=%fused_computation.clone | custom fusion | bytes 294912 | tf_op jit(solution)/shard_map/jit(_take)/gather | solution.py:22
  162.9 151.8 %gather_fusion.1 = s32[24576]{0:T(1024)S(1)} fusion(s32[192]{0:T(256)S(1)} %copy-done.2, s32[24576]{0:T(1024)S(1)} %fusion.5), kind=kCustom, calls=%fused_computation.1.clone | custom fusion | bytes 294912 | tf_op jit(solution)/shard_map/jit(_take)/gather | solution.py:22
  314.8 0.3 copy.25
  315.1 0.9 broadcast_multiply_fusion
  316.2 0.3 copy.24
  316.4 0.9 broadcast_multiply_fusion.1
  317.5 66.2 %all-gather.5.cloned.1.call-done = f32[6144,256]{0,1:T(8,128)} async-done(((f32[768,256]{0,1:T(8,128)}), f32[6144,256]{0,1:T(8,128)}) %all-gather.5.cloned.1.call-update) | async-done | bytes 6291472 | tf_op jit(solution)/shard_map/all_gather | solution.py:37
  383.7 3.8 dynamic-slice_select_fusion
  387.5 61.7 %all-gather.3.cloned.1.call-done = f32[6144,256]{0,1:T(8,128)} async-done(((f32[768,256]{0,1:T(8,128)}), f32[6144,256]{0,1:T(8,128)}) %all-gather.3.cloned.1.call-update) | async-done | bytes 6291472 | tf_op jit(solution)/shard_map/all_gather | solution.py:37
  449.2 3.9 dynamic-slice_select_fusion.1
  453.2 136.9 %all-reduce.9.cloned.1.call-done = (f32[3072,256]{0,1:T(8,128)}, f32[3072,256]{0,1:T(8,128)}) async-done(((f32[3072,256]{0,1:T(8,128)}, f32[3072,256]{0,1:T(8,128)}), (f32[3072,256]{0,1:T(8,128)}, f32[3072,256]{0,1:T(8,128)})) %all-reduce.9.cloned.1.call-update) | async-done | bytes 6291472 | tf_op jit(solution)/shard_map/psum | solution.py:14
  590.1 70.0 %convolution_bitcast_fusion.1 = f32[6144,256]{0,1:T(8,128)} fusion(f32[3072,256]{0,1:T(8,128)} %get-tuple-element.39, f32[6144,3072]{1,0:T(8,128)} %param.14), kind=kOutput, calls=%fused_computation.4 | convolution fusion | flops 57982058496 | bytes 84934656 | tf_op jit(solution)/shard_map/dot_general | solution.py:18
  660.4 1.6 copy-done.5
  662.0 70.3 %convolution_bitcast_fusion = f32[6144,256]{0,1:T(8,128)} fusion(f32[3072,256]{0,1:T(8,128)S(1)} %copy-done.5, f32[6144,3072]{1,0:T(8,128)} %param.14), kind=kOutput, calls=%fused_computation.3 | convolution fusion | flops 57982058496 | bytes 84934656 | tf_op jit(solution)/shard_map/dot_general | solution.py:18
  732.3 0.3 all-reduce.7.cloned.1.call-start
  732.6 1.3 multiply_negate_fusion
  733.9 1.5 fusion.11
  735.5 1.5 fusion.10
  737.0 64.8 %reduce-scatter.5.cloned.1.call-done = f32[768,256]{0,1:T(8,128)} async-done(((f32[6144,256]{0,1:T(8,128)}), f32[768,256]{0,1:T(8,128)}) %reduce-scatter.5.cloned.1.call-update) | async-done | bytes 786448 | tf_op jit(solution)/shard_map/reduce_scatter | solution.py:40
  801.8 2.7 fusion.12
  804.8 1.1 copy.30
  805.9 0.9 fusion.1
  806.8 1.1 copy.31
  808.0 129.5 %all-reduce.7.cloned.1.call-done = (f32[256,256]{1,0:T(8,128)}, f32[256,256]{1,0:T(8,128)}, f32[256,256]{0,1:T(8,128)}) async-done(((f32[256,256]{1,0:T(8,128)}, f32[256,256]{1,0:T(8,128)}, f32[256,256]{0,1:T(8,128)}), (f32[256,256]{1,0:T(8,128)}, f32[256,256]{1,0:T(8,128)}, f32[256,256]{0,1:T(8,128)})) %all-reduce.7.cloned.1.call-update) | async-done | bytes 786448 | tf_op jit(solution)/shard_map/psum | solution.py:71
  937.5 1.0 sub.20
  938.4 1.4 fusion.4
  939.9 0.6 fusion.3
  940.5 1.6 fusion.2
  942.1 0.8 copy.32
  (55 shorter events, 1.6 us)
Async XLA Ops:
  7.2 798.7 %copy-start = (f32[256,256]{1,0:T(8,128)S(1)}, f32[256,256]{1,0:T(8,128)}, u32[]{:S(2)}) copy-start(f32[256,256]{1,0:T(8,128)} %param.17) | copy-start | bytes 786436
  7.2 3.9 copy-start.1
  7.2 376.5 %all-gather.5.cloned.1.call-start = ((), (), s32[]{:S(2)}) async-start(), calls=%async_computation.4 | async-start | bytes 7077888 | tf_op jit(solution)/shard_map/all_gather | solution.py:37
  11.1 151.8 %copy-start.2 = (s32[192]{0:T(256)S(1)}, s32[192]{0:T(256)}, u32[]{:S(2)}) copy-start(s32[192]{0:T(256)} %param.21) | copy-start | bytes 2308
  162.9 151.8 %copy-start.9 = (f32[768,256]{1,0:T(8,128)S(1)}, f32[768,256]{1,0:T(8,128)}, u32[]{:S(2)}) copy-start(f32[768,256]{1,0:T(8,128)} %param.16) | copy-start | bytes 2359300
  314.8 1.4 copy-start.10
  316.1 133.1 %all-gather.3.cloned.1.call-start = ((), (), s32[]{:S(2)}) async-start(), calls=%async_computation.2 | async-start | bytes 7077888 | tf_op jit(solution)/shard_map/all_gather | solution.py:37
  317.4 272.7 %all-reduce.9.cloned.1.call-start = ((), (), s32[]{:S(2)}) async-start(), calls=%async_computation.7 | async-start | bytes 12582912 | tf_op jit(solution)/shard_map/psum | solution.py:14
  453.1 279.4 %reduce-scatter.3.cloned.1.call-start = ((), (), s32[]{:S(2)}) async-start(), calls=%async_computation.3 | async-start | bytes 7077888 | tf_op jit(solution)/shard_map/reduce_scatter | solution.py:40
  660.1 1.9 copy-start.5
  660.1 141.7 %reduce-scatter.5.cloned.1.call-start = ((), (), s32[]{:S(2)}) async-start(), calls=%async_computation.5 | async-start | bytes 7077888 | tf_op jit(solution)/shard_map/reduce_scatter | solution.py:40
  732.3 1.7 copy-start.3
  732.3 3.2 copy-start.4
  732.3 205.2 %all-reduce.7.cloned.1.call-start = ((), (), s32[]{:S(2)}) async-start(), calls=%async_computation.6 | async-start | bytes 1572864 | tf_op jit(solution)/shard_map/psum | solution.py:71
  733.9 70.7 %copy-start.12 = (f32[256,256]{1,0:T(8,128)S(1)}, f32[256,256]{1,0:T(8,128)}, u32[]{:S(2)}) copy-start(f32[256,256]{1,0:T(8,128)} %param.19) | copy-start | bytes 786436
  801.8 4.1 copy-start.6
  804.6 132.8 %copy-start.11 = (f32[256,256]{1,0:T(8,128)S(1)}, f32[256,256]{1,0:T(8,128)}, u32[]{:S(2)}) copy-start(f32[256,256]{1,0:T(8,128)} %param.18) | copy-start | bytes 786436
  938.4 4.5 copy-start.7
  939.9 3.1 copy-start.8
Sparse Core Ops, SparseCore 0:
  316.2 67.4 all-gather.4
  385.9 63.3 all-gather.2
  453.3 136.7 all-reduce.8
  660.2 69.7 reduce-scatter.2
  732.4 69.4 reduce-scatter.4
  807.8 129.6 all-reduce.6
where the time goes:
time: 950 us
  waiting for transfers between devices  459 us (48%)
  local copies, waits for them, and re-layouts  310 us (33%)
  matrix products  151 us (16%)
  other arithmetic  15.3 us (2%)
  between operations  14.4 us (2%)
    gather x2, local copies, waits for them, and re-layouts, local_mask(): flags = jnp.repeat(blocks, BLK, total_repeat_length=blocks.shape[0] * BLK)  304 us
    dot_general x9, matrix products, matmul(): jnp.dot(left, right, precision=HIGHEST, preferred_element_type=jnp.float32)  151 us
    psum x1, waiting for transfers between devices, spread(): return lax.psum(kept, axis)  137 us
    psum x1, waiting for transfers between devices, per_device(): lax.psum((parent_local, cross_local, image_local), ('row', 'col'))  129 us
    all_gather x2, waiting for transfers between devices, apply_inverse(): block_rows = lax.all_gather(panel, 'col', axis=0, tiled=True)  128 us
    reduce_scatter x2, waiting for transfers between devices, apply_inverse(): lax.psum_scatter(matmul(lax.slice_in_dim(inverse, 0, rows_here * lax.axis...  64.9 us
  transfers between devices with their start and end apart: 6, of which 5 were waited for; matrix products, arithmetic and copies ran while one was open for 9% of the time, Pallas kernels for 0%

commit v1 on v0

v1 whole, which is shorter than its diff:
```python
import functools

import jax
import jax.numpy as jnp
from jax import lax
from jax.experimental import pallas as pl
from jax.experimental.pallas import tpu as pltpu
from jax.sharding import PartitionSpec as P

BLK = 128
GROUP = 4
BOTH = ("row", "col")


def matmul(left, right):
    return jnp.dot(
        left, right, precision=lax.Precision.HIGH, preferred_element_type=jnp.float32
    )


def local_mask(blocks, rows_here):
    flags = jnp.broadcast_to(blocks[:, None], (blocks.shape[0], BLK)).reshape(-1)
    device = lax.axis_index("row") * lax.axis_size("col") + lax.axis_index("col")
    return lax.dynamic_slice_in_dim(flags, device * rows_here, rows_here, 0)[:, None] > 0


def product_kernel(
    row_flags, col_flags, inverse, panel, out, rows, cols, held, high, low, total, in_sems, out_sems
):
    def listed(flags, places):
        def step(i, count):
            places[count] = i
            return count + flags[i]

        return lax.fori_loop(0, flags.shape[0], step, 0)

    n_rows = listed(row_flags, rows)
    n_cols = listed(col_flags, cols)
    groups = (n_rows + GROUP - 1) // GROUP
    pairs = (n_cols + 1) // 2

    def fetch(group, q, slot):
        place = rows[jnp.minimum(group * GROUP + q, n_rows - 1)]
        return pltpu.make_async_copy(
            inverse.at[pl.ds(pl.multiple_of(place * BLK, BLK), BLK), :],
            held.at[slot, pl.ds(q * BLK, BLK), :],
            in_sems.at[slot, q],
        )

    def put(group, q, slot):
        place = rows[jnp.minimum(group * GROUP + q, n_rows - 1)]
        return pltpu.make_async_copy(
            total.at[slot, pl.ds(q * BLK, BLK), :],
            out.at[pl.ds(pl.multiple_of(place * BLK, BLK), BLK), :],
            out_sems.at[slot, q],
        )

    def each(group, act):
        for q in range(GROUP):

            @pl.when((group >= 0) & (group * GROUP + q < n_rows))
            def _():
                act(q)

    each(0, lambda q: fetch(0, q, 0).start())

    def split(t, carry):
        place = pl.multiple_of(cols[t] * BLK, BLK)
        block = panel[pl.ds(place, BLK), :]
        top = block.astype(jnp.bfloat16)
        here = pl.ds(pl.multiple_of(t * BLK, BLK), BLK)
        high[here, :] = top
        low[here, :] = (block - top.astype(jnp.float32)).astype(jnp.bfloat16)
        return carry

    lax.fori_loop(0, n_cols, split, 0)
    tail = pl.ds(pl.multiple_of(n_cols * BLK, BLK), BLK)
    high[tail, :] = jnp.zeros((BLK, high.shape[1]), jnp.bfloat16)
    low[tail, :] = jnp.zeros((BLK, low.shape[1]), jnp.bfloat16)
    cols[n_cols] = 0

    def one_group(group, carry):
        slot = lax.rem(group, 2)
        each(group + 1, lambda q: fetch(group + 1, q, 1 - slot).start())
        each(group - 2, lambda q: put(group - 2, q, slot).wait())
        each(group, lambda q: fetch(group, q, slot).wait())
        total[slot] = jnp.zeros(total.shape[1:], jnp.float32)

        def one_pair(pair, inner):
            first = pl.multiple_of(cols[2 * pair] * BLK, BLK)
            second = pl.multiple_of(cols[2 * pair + 1] * BLK, BLK)
            left = jnp.concatenate(
                [held[slot, :, pl.ds(first, BLK)], held[slot, :, pl.ds(second, BLK)]], axis=1
            )
            left_high = left.astype(jnp.bfloat16)
            left_low = (left - left_high.astype(jnp.float32)).astype(jnp.bfloat16)
            here = pl.ds(pl.multiple_of(pair * 2 * BLK, 2 * BLK), 2 * BLK)
            right_high = high[here, :]
            right_low = low[here, :]
            dot = functools.partial(jnp.dot, preferred_element_type=jnp.float32)
            total[slot] += (
                dot(left_high, right_high) + dot(left_low, right_high) + dot(left_high, right_low)
            )
            return inner

        lax.fori_loop(0, pairs, one_pair, 0)
        each(group, lambda q: put(group, q, slot).start())
        return carry

    lax.fori_loop(0, groups, one_group, 0)
    for back in (2, 1):
        last = groups - back
        each(last, lambda q: put(last, q, lax.rem(jnp.maximum(last, 0), 2)).wait())


def product(inverse, panel, blocks):
    height, width = inverse.shape
    tall, wide = height // BLK, width // BLK
    row_flags = lax.dynamic_slice_in_dim(blocks, lax.axis_index("row") * tall, tall, 0)
    col_flags = lax.dynamic_slice_in_dim(blocks, lax.axis_index("col") * wide, wide, 0)
    across = panel.shape[1]
    return pl.pallas_call(
        product_kernel,
        out_shape=jax.ShapeDtypeStruct((height, across), jnp.float32),
        in_specs=[
            pl.BlockSpec(memory_space=pltpu.SMEM),
            pl.BlockSpec(memory_space=pltpu.SMEM),
            pl.BlockSpec(memory_space=pl.ANY),
            pl.BlockSpec(memory_space=pltpu.VMEM),
        ],
        out_specs=pl.BlockSpec(memory_space=pl.ANY),
        scratch_shapes=[
            pltpu.SMEM((tall + 1,), jnp.int32),
            pltpu.SMEM((wide + 1,), jnp.int32),
            pltpu.VMEM((2, GROUP * BLK, width), jnp.float32),
            pltpu.VMEM((width + BLK, across), jnp.bfloat16),
            pltpu.VMEM((width + BLK, across), jnp.bfloat16),
            pltpu.VMEM((2, GROUP * BLK, across), jnp.float32),
            pltpu.SemaphoreType.DMA((2, GROUP)),
            pltpu.SemaphoreType.DMA((2, GROUP)),
        ],
        compiler_params=pltpu.CompilerParams(vmem_limit_bytes=40 * 2**20),
        cost_estimate=pl.CostEstimate(
            flops=3 * height * width * across, bytes_accessed=height * width * 2, transcendentals=0
        ),
    )(row_flags, col_flags, inverse, panel)


def column_rows(panel):
    n_row, n_col = lax.axis_size("row"), lax.axis_size("col")
    routes = [(k, k % n_row * n_col + k // n_row) for k in range(n_row * n_col)]
    moved = lax.ppermute(panel, BOTH, routes)
    return lax.all_gather(moved, "row", axis=0, tiled=True)


def summed_rows(partial, rows_here):
    n_col = lax.axis_size("col")
    chips = n_col // 2
    index = lax.axis_index("col")
    chip, core = index // 2, index % 2
    step = 1 - 2 * core
    parts = partial.reshape(chips, 2, rows_here, partial.shape[1])
    theirs = lax.dynamic_index_in_dim(parts, 1 - core, 1, keepdims=False)
    mine = lax.dynamic_index_in_dim(parts, core, 1, keepdims=False)
    got = lax.ppermute(theirs, "col", [(k, k ^ 1) for k in range(n_col)])
    ring = [((2 * z + c), (z + 1 - 2 * c) % chips * 2 + c) for z in range(chips) for c in (0, 1)]

    def term(s):
        place = (chip - step * (s + 1) + 2 * chips * (s + 1)) % chips
        return lax.dynamic_index_in_dim(mine, place, 0, keepdims=False) + (
            lax.dynamic_index_in_dim(got, place, 0, keepdims=False)
        )

    running = term(0)
    for s in range(1, chips):
        running = lax.ppermute(running, "col", ring) + term(s)
    return running


def total_of(value):
    devices = lax.axis_size("row") * lax.axis_size("col")
    bit = 1
    while bit < devices:
        value = value + lax.ppermute(value, BOTH, [(k, k ^ bit) for k in range(devices)])
        bit *= 2
    return value


def per_device(
    inverse,
    parent_panel,
    child_panel,
    child_top,
    diag_parent,
    diag_child,
    parent_blocks,
    child_blocks,
):
    rows_here = parent_panel.shape[0]
    parent_mask = local_mask(parent_blocks, rows_here)
    child_mask = local_mask(child_blocks, rows_here)
    parent_masked = jnp.where(parent_mask, parent_panel, 0)
    child_masked = jnp.where(child_mask, child_panel, 0)
    parent_rows = column_rows(parent_panel)
    child_rows = column_rows(child_panel)
    parent_partial = product(inverse, parent_rows, parent_blocks)
    child_partial = product(inverse, child_rows, child_blocks)
    parent_column = jnp.where(parent_mask, -summed_rows(parent_partial, rows_here), 0)
    child_image = jnp.where(child_mask, summed_rows(child_partial, rows_here), 0)
    parent_local = matmul(parent_masked.T, parent_column)
    cross_local = matmul(parent_column.T, child_masked)
    carried = matmul(parent_column, child_top)
    child_column = jnp.where(child_mask, -(carried + child_image), 0)
    image_local = matmul(child_masked.T, child_image)
    first_sums = total_of(jnp.stack([parent_local, cross_local]))
    parent_sum, cross_sum = first_sums[0], first_sums[1]
    image_sum = total_of(image_local)
    parent_diagonal = diag_parent - parent_sum
    child_upper = -(matmul(parent_diagonal, child_top) + cross_sum)
    child_diagonal = (
        diag_child - matmul(child_top.T, child_upper) + matmul(cross_sum.T, child_top) + image_sum
    )
    return (parent_column, parent_diagonal, child_column, child_upper, child_diagonal)


def solution(mesh):
    placed = (
        P("row", "col"),
        P(("row", "col"), None),
        P(("row", "col"), None),
        P(),
        P(),
        P(),
        P(),
        P(),
    )
    return jax.shard_map(
        per_device,
        mesh=mesh,
        in_specs=placed,
        out_specs=(P(("row", "col"), None), P(), P(("row", "col"), None), P(), P()),
        check_vma=False,
    )
```

time: 950 us -> 414 us (0.44)
  local copies, waits for them, and re-layouts: 310 us -> 15.6 us
  waiting for transfers between devices: 459 us -> 268 us
  matrix products: 151 us -> 5.22 us
  Pallas kernels: 0 us -> 67.8 us
  starting transfers between devices: 0.65 us -> 33.7 us
    gather x2 -> x0, local copies, waits for them, and re-layouts: 304 us -> none  [local_mask(): flags = jnp.repeat(blocks, BLK, total_repeat_length=blocks.shape[0] * BLK)]
    psum x2 -> x0, waiting for transfers between devices: 266 us -> none  [the longest x1 137 us: spread(): return lax.psum(kept, axis)]
    dot_general x9 -> x7, matrix products: 151 us -> 5.22 us  [matmul(): jnp.dot(left, right, precision=lax.Precision.HIGH, preferred_element_type...]
    ppermute x0 -> x20, waiting for transfers between devices: none -> 135 us  [the longest x6 99.1 us: summed_rows(): running = lax.ppermute(running, 'col', ring) + term(s)]
    pallas_call x0 -> x2, Pallas kernels: none -> 67.8 us  [product(): pl.pallas_call(product_kernel, out_shape=jax.ShapeDtypeStruct((height, ac...]
    reduce_scatter x2 -> x0, waiting for transfers between devices: 64.9 us -> none  [apply_inverse(): lax.psum_scatter(matmul(lax.slice_in_dim(inverse, 0, rows_here * lax.axis...]
    ppermute x0 -> x20, starting transfers between devices: none -> 33.6 us  [the longest x10 22.8 us: total_of(): lax.ppermute(value, BOTH, [(k, k ^ bit) for k in range(devices)])]
    add x0 -> x15, other arithmetic: none -> 11.6 us  [the longest x4 6.33 us: summed_rows(): running = lax.ppermute(running, 'col', ring) + term(s)]
  transfers between devices with their start and end apart: 6 -> 22, of which waited for: 5 -> 15; matrix products, arithmetic and copies ran while one was open for 9% -> 6% of each run, Pallas kernels for 0% -> 16%
where the time goes in v1:
time: 414 us; the launch traced here: 419 us
  waiting for transfers between devices  268 us (65%)
  Pallas kernels  67.8 us (16%)
  starting transfers between devices  33.7 us (8%)
  local copies, waits for them, and re-layouts  15.6 us (4%)
  other arithmetic  15 us (4%)
  between operations  14.4 us (3%)
  matrix products  5.22 us (1%)
    all_gather x2, waiting for transfers between devices, column_rows(): return lax.all_gather(moved, 'row', axis=0, tiled=True)  133 us
    ppermute x6, waiting for transfers between devices, summed_rows(): running = lax.ppermute(running, 'col', ring) + term(s)  99.1 us
    pallas_call x2, Pallas kernels, product(): pl.pallas_call(product_kernel, out_shape=jax.ShapeDtypeStruct((height, ac...  67.8 us
    ppermute x10, waiting for transfers between devices, total_of(): lax.ppermute(value, BOTH, [(k, k ^ bit) for k in range(devices)])  35.9 us
    ppermute x10, starting transfers between devices, total_of(): lax.ppermute(value, BOTH, [(k, k ^ bit) for k in range(devices)])  22.8 us
    unnamed x32, local copies, waits for them, and re-layouts  11.6 us
  transfers between devices with their start and end apart: 22, of which 15 were waited for; matrix products, arithmetic and copies ran while one was open for 6% of the time, Pallas kernels for 16%

profile of v1, /device:TPU:0, one launch (start us, length us, event | category | flops | bytes accessed | tf_op | source)
XLA Modules:
  0.0 419.5 jit_solution(14528595638570489772)
XLA Ops:
  7.2 1.9 collective-permute-start
  10.1 1.8 collective-permute-start.10
  14.3 132.7 %all-gather.3.cloned.1.call-done.panel = f32[3072,256]{1,0:T(8,128)} async-done(((f32[768,256]{1,0:T(8,128)}), f32[3072,256]{1,0:T(8,128)}) %all-gather.3.cloned.1.call-update) | async-done | bytes 3145744 | tf_op jit(solution)/shard_map/all_gather | solution.py:153
  147.1 1.9 copy-done.3
  148.9 49.6 %shard_map.119 = f32[6144,256]{1,0:T(8,128)S(1)} custom-call(s32[48]{0:T(128)S(1)} %dynamic_slice.77.row_flags, s32[24]{0:T(128)S(1)} %dynamic_slice.78.col_flags, f32[6144,3072]{1,0:T(8,128)} %inverse.3, f32[3072,256]{1,0:T(8,128)S(1)} %copy-done.3), custom_call_target="tpu_custom_call" | custom-call | flops 14495514624 | bytes 37748736 | tf_op jit(solution)/shard_map/pallas_call | solution.py:122
  198.6 2.0 dynamic-slice_bitcast_fusion.1
  200.6 1.6 copy-done.2
  202.4 1.9 copy-done.4
  204.3 18.2 %shard_map.120 = f32[6144,256]{1,0:T(8,128)S(1)} custom-call(s32[48]{0:T(128)S(1)} %dynamic_slice.89.row_flags, s32[24]{0:T(128)S(1)} %dynamic_slice.90.col_flags, f32[6144,3072]{1,0:T(8,128)} %inverse.3, f32[3072,256]{1,0:T(8,128)S(1)} %copy-done.4), custom_call_target="tpu_custom_call" | custom-call | flops 14495514624 | bytes 37748736 | tf_op jit(solution)/shard_map/pallas_call | solution.py:122
  222.8 2.4 copy-done.1
  225.2 6.3 %collective-permute-start.11 = (f32[4,768,256]{2,1,0:T(8,128)S(1)}, f32[4,768,256]{2,1,0:T(8,128)}, u32[]{:S(2)}, u32[]{:S(2)}) collective-permute-start(f32[4,768,256]{2,1,0:T(8,128)S(1)} %dynamic-slice_bitcast_fusion), channel_id=1, source_target_pairs={{0,1},{1,0},{2,3},{3,2},{4,5},{5,4},{6,7},{7,6},{8,9},{9,8},{10,11... | collective-permute-start | bytes 9437192 | tf_op jit(solution)/shard_map/ppermute | solution.py:165
  231.5 2.4 bitcast_add_fusion.7
  233.9 21.4 %collective-permute-done.2 = f32[768,256]{1,0:T(8,128)} collective-permute-done((f32[768,256]{1,0:T(8,128)}, f32[768,256]{1,0:T(8,128)}, u32[]{:S(2)}, u32[]{:S(2)}) %collective-permute-start.2) | collective-permute-done | bytes 786464 | tf_op jit(solution)/shard_map/ppermute | solution.py:176
  255.3 1.8 fusion.13
  259.3 20.0 %collective-permute-done.3 = f32[768,256]{1,0:T(8,128)S(1)} collective-permute-done((f32[768,256]{1,0:T(8,128)S(1)}, f32[768,256]{1,0:T(8,128)S(1)}, u32[]{:S(2)}, u32[]{:S(2)}) %collective-permute-start.3) | collective-permute-done | bytes 786464 | tf_op jit(solution)/shard_map/ppermute | solution.py:176
  281.1 15.1 %collective-permute-done.12 = f32[768,256]{1,0:T(8,128)S(1)} collective-permute-done((f32[768,256]{1,0:T(8,128)S(1)}, f32[768,256]{1,0:T(8,128)S(1)}, u32[]{:S(2)}, u32[]{:S(2)}) %collective-permute-start.12) | collective-permute-done | bytes 786464 | tf_op jit(solution)/shard_map/ppermute | solution.py:176
  297.8 15.2 %collective-permute-done.4 = f32[768,256]{1,0:T(8,128)S(1)} collective-permute-done((f32[768,256]{1,0:T(8,128)S(1)}, f32[768,256]{1,0:T(8,128)S(1)}, u32[]{:S(2)}, u32[]{:S(2)}) %collective-permute-start.4) | collective-permute-done | bytes 786464 | tf_op jit(solution)/shard_map/ppermute | solution.py:176
  316.6 1.9 collective-permute-done.5
  318.7 11.2 %collective-permute-done.13 = f32[768,256]{1,0:T(8,128)S(1)} collective-permute-done((f32[768,256]{1,0:T(8,128)S(1)}, f32[768,256]{1,0:T(8,128)S(1)}, u32[]{:S(2)}, u32[]{:S(2)}) %collective-permute-start.13) | collective-permute-done | bytes 786464 | tf_op jit(solution)/shard_map/ppermute | solution.py:176
  331.5 5.8 %collective-permute-done.6 = f32[2,256,256]{2,1,0:T(8,128)S(1)} collective-permute-done((f32[2,256,256]{2,1,0:T(8,128)S(1)}, f32[2,256,256]{2,1,0:T(8,128)S(1)}, u32[]{:S(2)}, u32[]{:S(2)}) %collective-permute-start.6) | collective-permute-done | bytes 524320 | tf_op jit(solution)/shard_map/ppermute | solution.py:184
  337.4 4.5 %collective-permute-start.7 = (f32[2,256,256]{2,1,0:T(8,128)S(1)}, f32[2,256,256]{2,1,0:T(8,128)S(1)}, u32[]{:S(2)}, u32[]{:S(2)}) collective-permute-start(f32[2,256,256]{2,1,0:T(8,128)S(1)} %fusion.39), channel_id=1, source_target_pairs={{0,4},{1,5},{2,6},{3,7},{4,0},{5,1},{6,2},{7,3},{8,12},{9,13},{10,... | collective-permute-start | bytes 1572872 | tf_op jit(solution)/shard_map/ppermute | solution.py:184
  341.8 16.1 %collective-permute-done.14 = f32[768,256]{1,0:T(8,128)S(1)} collective-permute-done((f32[768,256]{1,0:T(8,128)S(1)}, f32[768,256]{1,0:T(8,128)S(1)}, u32[]{:S(2)}, u32[]{:S(2)}) %collective-permute-start.14) | collective-permute-done | bytes 786464 | tf_op jit(solution)/shard_map/ppermute | solution.py:176
  358.0 1.6 fusion.6
  361.9 9.2 %collective-permute-done.7 = f32[2,256,256]{2,1,0:T(8,128)S(1)} collective-permute-done((f32[2,256,256]{2,1,0:T(8,128)S(1)}, f32[2,256,256]{2,1,0:T(8,128)S(1)}, u32[]{:S(2)}, u32[]{:S(2)}) %collective-permute-start.7) | collective-permute-done | bytes 524320 | tf_op jit(solution)/shard_map/ppermute | solution.py:184
  371.4 2.2 collective-permute-start.16
  373.6 5.0 %collective-permute-done.16 = f32[256,256]{0,1:T(8,128)S(1)} collective-permute-done((f32[256,256]{0,1:T(8,128)S(1)}, f32[256,256]{0,1:T(8,128)S(1)}, u32[]{:S(2)}, u32[]{:S(2)}) %collective-permute-start.16) | collective-permute-done | bytes 262176 | tf_op jit(solution)/shard_map/ppermute | solution.py:184
  378.6 4.4 %collective-permute-start.17 = (f32[256,256]{0,1:T(8,128)S(1)}, f32[256,256]{0,1:T(8,128)}, u32[]{:S(2)}, u32[]{:S(2)}) collective-permute-start(f32[256,256]{0,1:T(8,128)S(1)} %add.247), channel_id=1, source_target_pairs={{0,4},{1,5},{2,6},{3,7},{4,0},{5,1},{6,2},{7,3},{8,12},{9,13},{10,... | collective-permute-start | bytes 786440 | tf_op jit(solution)/shard_map/ppermute | solution.py:184
  383.4 5.0 %collective-permute-start.9 = (f32[2,256,256]{2,1,0:T(8,128)S(1)}, f32[2,256,256]{2,1,0:T(8,128)S(1)}, u32[]{:S(2)}, u32[]{:S(2)}) collective-permute-start(f32[2,256,256]{2,1,0:T(8,128)S(1)} %add.234), channel_id=1, source_target_pairs={{0,16},{1,17},{2,18},{3,19},{4,20},{5,21},{6,22},{7,23},{8,24},{9,... | collective-permute-start | bytes 1572872 | tf_op jit(solution)/shard_map/ppermute | solution.py:184
  389.4 3.1 collective-permute-done.17
  395.0 6.3 %collective-permute-done.18 = f32[256,256]{0,1:T(8,128)S(1)} collective-permute-done((f32[256,256]{0,1:T(8,128)S(1)}, f32[256,256]{0,1:T(8,128)S(1)}, u32[]{:S(2)}, u32[]{:S(2)}) %collective-permute-start.18) | collective-permute-done | bytes 262176 | tf_op jit(solution)/shard_map/ppermute | solution.py:184
  401.3 5.0 %collective-permute-start.19 = (f32[256,256]{0,1:T(8,128)S(1)}, f32[256,256]{0,1:T(8,128)S(1)}, u32[]{:S(2)}, u32[]{:S(2)}) collective-permute-start(f32[256,256]{0,1:T(8,128)S(1)} %add.249), channel_id=1, source_target_pairs={{0,16},{1,17},{2,18},{3,19},{4,20},{5,21},{6,22},{7,23},{8,24},{9,... | collective-permute-start | bytes 786440 | tf_op jit(solution)/shard_map/ppermute | solution.py:184
  407.1 4.3 %collective-permute-done.19 = f32[256,256]{0,1:T(8,128)S(1)} collective-permute-done((f32[256,256]{0,1:T(8,128)S(1)}, f32[256,256]{0,1:T(8,128)S(1)}, u32[]{:S(2)}, u32[]{:S(2)}) %collective-permute-start.19) | collective-permute-done | bytes 262176 | tf_op jit(solution)/shard_map/ppermute | solution.py:184
  (84 shorter events, 23.2 us)
Async XLA Ops:
  7.2 386.4 %copy-start = (f32[256,256]{1,0:T(8,128)S(1)}, f32[256,256]{1,0:T(8,128)}, u32[]{:S(2)}) copy-start(f32[256,256]{1,0:T(8,128)} %param.11) | copy-start | bytes 786436
  7.2 139.9 %all-gather.3.cloned.1.call-start = ((), (), s32[]{:S(2)}) async-start(), calls=%async_computation | async-start | bytes 3932160 | tf_op jit(solution)/shard_map/all_gather | solution.py:153
  7.2 1.9 collective-permute-start
  10.1 192.3 %all-gather.5.cloned.1.call-start = ((), (), s32[]{:S(2)}) async-start(), calls=%async_computation.1 | async-start | bytes 3932160 | tf_op jit(solution)/shard_map/all_gather | solution.py:153
  10.1 1.8 collective-permute-start.10
  198.5 3.7 copy-start.2
  198.5 3.7 copy-start.13
  202.2 29.3 %collective-permute-start.1 = (f32[4,768,256]{2,1,0:T(8,128)}, f32[4,768,256]{2,1,0:T(8,128)}, u32[]{:S(2)}, u32[]{:S(2)}) collective-permute-start(f32[4,768,256]{2,1,0:T(8,128)} %dynamic-slice_bitcast_fusion.1), channel_id=1, source_target_pairs={{0,1},{1,0},{2,3},{3,2},{4,5},{5,4},{6,7},{7,6},{8,9},{9,8},{10,11... | collective-permute-start | bytes 9437192 | tf_op jit(solution)/shard_map/ppermute | solution.py:165
  225.2 32.1 %collective-permute-start.11 = (f32[4,768,256]{2,1,0:T(8,128)S(1)}, f32[4,768,256]{2,1,0:T(8,128)}, u32[]{:S(2)}, u32[]{:S(2)}) collective-permute-start(f32[4,768,256]{2,1,0:T(8,128)S(1)} %dynamic-slice_bitcast_fusion), channel_id=1, source_target_pairs={{0,1},{1,0},{2,3},{3,2},{4,5},{5,4},{6,7},{7,6},{8,9},{9,8},{10,11... | collective-permute-start | bytes 9437192 | tf_op jit(solution)/shard_map/ppermute | solution.py:165
  233.9 21.4 %collective-permute-start.2 = (f32[768,256]{1,0:T(8,128)}, f32[768,256]{1,0:T(8,128)}, u32[]{:S(2)}, u32[]{:S(2)}) collective-permute-start(f32[768,256]{1,0:T(8,128)} %bitcast_add_fusion.7), channel_id=1, source_target_pairs={{0,2},{1,7},{2,4},{3,1},{4,6},{5,3},{6,0},{7,5},{8,10},{9,15},{10,... | collective-permute-start | bytes 2359304 | tf_op jit(solution)/shard_map/ppermute | solution.py:176
  257.0 23.9 %copy-start.14 = (s32[192]{0:T(256)S(1)}, s32[192]{0:T(256)}, u32[]{:S(2)}) copy-start(s32[192]{0:T(256)} %param.14) | copy-start | bytes 2308
  257.0 22.3 %collective-permute-start.3 = (f32[768,256]{1,0:T(8,128)S(1)}, f32[768,256]{1,0:T(8,128)S(1)}, u32[]{:S(2)}, u32[]{:S(2)}) collective-permute-start(f32[768,256]{1,0:T(8,128)S(1)} %fusion.13), channel_id=1, source_target_pairs={{0,2},{1,7},{2,4},{3,1},{4,6},{5,3},{6,0},{7,5},{8,10},{9,15},{10,... | collective-permute-start | bytes 2359304 | tf_op jit(solution)/shard_map/ppermute | solution.py:176
  258.8 37.4 %collective-permute-start.12 = (f32[768,256]{1,0:T(8,128)S(1)}, f32[768,256]{1,0:T(8,128)S(1)}, u32[]{:S(2)}, u32[]{:S(2)}) collective-permute-start(f32[768,256]{1,0:T(8,128)S(1)} %bitcast_add_fusion.3), channel_id=1, source_target_pairs={{0,2},{1,7},{2,4},{3,1},{4,6},{5,3},{6,0},{7,5},{8,10},{9,15},{10,... | collective-permute-start | bytes 2359304 | tf_op jit(solution)/shard_map/ppermute | solution.py:176
  280.8 32.2 %collective-permute-start.4 = (f32[768,256]{1,0:T(8,128)S(1)}, f32[768,256]{1,0:T(8,128)S(1)}, u32[]{:S(2)}, u32[]{:S(2)}) collective-permute-start(f32[768,256]{1,0:T(8,128)S(1)} %fusion.12), channel_id=1, source_target_pairs={{0,2},{1,7},{2,4},{3,1},{4,6},{5,3},{6,0},{7,5},{8,10},{9,15},{10,... | collective-permute-start | bytes 2359304 | tf_op jit(solution)/shard_map/ppermute | solution.py:176
  281.1 33.5 %copy-start.9 = (f32[768,256]{1,0:T(8,128)S(1)}, f32[768,256]{1,0:T(8,128)}, u32[]{:S(2)}) copy-start(f32[768,256]{1,0:T(8,128)} %param.9) | copy-start | bytes 2359300
  297.7 17.9 %copy-start.6 = (f32[768,256]{1,0:T(8,128)S(1)}, f32[768,256]{1,0:T(8,128)}, u32[]{:S(2)}) copy-start(f32[768,256]{1,0:T(8,128)} %param.10) | copy-start | bytes 2359300
  297.7 32.2 %collective-permute-start.13 = (f32[768,256]{1,0:T(8,128)S(1)}, f32[768,256]{1,0:T(8,128)S(1)}, u32[]{:S(2)}, u32[]{:S(2)}) collective-permute-start(f32[768,256]{1,0:T(8,128)S(1)} %fusion.8), channel_id=1, source_target_pairs={{0,2},{1,7},{2,4},{3,1},{4,6},{5,3},{6,0},{7,5},{8,10},{9,15},{10,... | collective-permute-start | bytes 2359304 | tf_op jit(solution)/shard_map/ppermute | solution.py:176
  314.6 79.0 %copy-start.5 = (f32[768,256]{1,0:T(8,128)}, f32[768,256]{1,0:T(8,128)S(1)}, u32[]{:S(2)}) copy-start(f32[768,256]{1,0:T(8,128)S(1)} %fusion.11) | copy-start | bytes 2359300
  316.6 2.0 collective-permute-start.5
  318.6 18.7 %collective-permute-start.6 = (f32[2,256,256]{2,1,0:T(8,128)S(1)}, f32[2,256,256]{2,1,0:T(8,128)S(1)}, u32[]{:S(2)}, u32[]{:S(2)}) collective-permute-start(f32[2,256,256]{2,1,0:T(8,128)S(1)} %fusion.28), channel_id=1, source_target_pairs={{0,2},{1,3},{2,0},{3,1},{4,6},{5,7},{6,4},{7,5},{8,10},{9,11},{10,... | collective-permute-start | bytes 1572872 | tf_op jit(solution)/shard_map/ppermute | solution.py:184
  331.4 26.6 %collective-permute-start.14 = (f32[768,256]{1,0:T(8,128)S(1)}, f32[768,256]{1,0:T(8,128)S(1)}, u32[]{:S(2)}, u32[]{:S(2)}) collective-permute-start(f32[768,256]{1,0:T(8,128)S(1)} %fusion.7), channel_id=1, source_target_pairs={{0,2},{1,7},{2,4},{3,1},{4,6},{5,3},{6,0},{7,5},{8,10},{9,15},{10,... | collective-permute-start | bytes 2359304 | tf_op jit(solution)/shard_map/ppermute | solution.py:176
  337.4 33.8 %collective-permute-start.7 = (f32[2,256,256]{2,1,0:T(8,128)S(1)}, f32[2,256,256]{2,1,0:T(8,128)S(1)}, u32[]{:S(2)}, u32[]{:S(2)}) collective-permute-start(f32[2,256,256]{2,1,0:T(8,128)S(1)} %fusion.39), channel_id=1, source_target_pairs={{0,4},{1,5},{2,6},{3,7},{4,0},{5,1},{6,2},{7,3},{8,12},{9,13},{10,... | collective-permute-start | bytes 1572872 | tf_op jit(solution)/shard_map/ppermute | solution.py:184
  360.5 10.8 %collective-permute-start.15 = (f32[256,256]{0,1:T(8,128)S(1)}, f32[256,256]{0,1:T(8,128)S(1)}, u32[]{:S(2)}, u32[]{:S(2)}) collective-permute-start(f32[256,256]{0,1:T(8,128)S(1)} %fusion.15), channel_id=1, source_target_pairs={{0,1},{1,0},{2,3},{3,2},{4,5},{5,4},{6,7},{7,6},{8,9},{9,8},{10,11... | collective-permute-start | bytes 786440 | tf_op jit(solution)/shard_map/ppermute | solution.py:184
  371.2 12.0 %collective-permute-start.8 = (f32[2,256,256]{2,1,0:T(8,128)S(1)}, f32[2,256,256]{2,1,0:T(8,128)S(1)}, u32[]{:S(2)}, u32[]{:S(2)}) collective-permute-start(f32[2,256,256]{2,1,0:T(8,128)S(1)} %add.233), channel_id=1, source_target_pairs={{0,8},{1,9},{2,10},{3,11},{4,12},{5,13},{6,14},{7,15},{8,0},{9,1},... | collective-permute-start | bytes 1572872 | tf_op jit(solution)/shard_map/ppermute | solution.py:184
  371.4 7.2 %collective-permute-start.16 = (f32[256,256]{0,1:T(8,128)S(1)}, f32[256,256]{0,1:T(8,128)S(1)}, u32[]{:S(2)}, u32[]{:S(2)}) collective-permute-start(f32[256,256]{0,1:T(8,128)S(1)} %add.246), channel_id=1, source_target_pairs={{0,2},{1,3},{2,0},{3,1},{4,6},{5,7},{6,4},{7,5},{8,10},{9,11},{10,... | collective-permute-start | bytes 786440 | tf_op jit(solution)/shard_map/ppermute | solution.py:184
  378.6 13.9 %collective-permute-start.17 = (f32[256,256]{0,1:T(8,128)S(1)}, f32[256,256]{0,1:T(8,128)}, u32[]{:S(2)}, u32[]{:S(2)}) collective-permute-start(f32[256,256]{0,1:T(8,128)S(1)} %add.247), channel_id=1, source_target_pairs={{0,4},{1,5},{2,6},{3,7},{4,0},{5,1},{6,2},{7,3},{8,12},{9,13},{10,... | collective-permute-start | bytes 786440 | tf_op jit(solution)/shard_map/ppermute | solution.py:184
  383.4 22.9 %collective-permute-start.9 = (f32[2,256,256]{2,1,0:T(8,128)S(1)}, f32[2,256,256]{2,1,0:T(8,128)S(1)}, u32[]{:S(2)}, u32[]{:S(2)}) collective-permute-start(f32[2,256,256]{2,1,0:T(8,128)S(1)} %add.234), channel_id=1, source_target_pairs={{0,16},{1,17},{2,18},{3,19},{4,20},{5,21},{6,22},{7,23},{8,24},{9,... | collective-permute-start | bytes 1572872 | tf_op jit(solution)/shard_map/ppermute | solution.py:184
  389.4 16.9 %copy-start.12 = (f32[256,256]{1,0:T(8,128)S(1)}, f32[256,256]{1,0:T(8,128)}, u32[]{:S(2)}) copy-start(f32[256,256]{1,0:T(8,128)} %param.12) | copy-start | bytes 786436
  393.5 7.8 %collective-permute-start.18 = (f32[256,256]{0,1:T(8,128)S(1)}, f32[256,256]{0,1:T(8,128)S(1)}, u32[]{:S(2)}, u32[]{:S(2)}) collective-permute-start(f32[256,256]{0,1:T(8,128)S(1)} %add.248), channel_id=1, source_target_pairs={{0,8},{1,9},{2,10},{3,11},{4,12},{5,13},{6,14},{7,15},{8,0},{9,1},... | collective-permute-start | bytes 786440 | tf_op jit(solution)/shard_map/ppermute | solution.py:184
  401.3 10.1 %collective-permute-start.19 = (f32[256,256]{0,1:T(8,128)S(1)}, f32[256,256]{0,1:T(8,128)S(1)}, u32[]{:S(2)}, u32[]{:S(2)}) collective-permute-start(f32[256,256]{0,1:T(8,128)S(1)} %add.249), channel_id=1, source_target_pairs={{0,16},{1,17},{2,18},{3,19},{4,20},{5,21},{6,22},{7,23},{8,24},{9,... | collective-permute-start | bytes 786440 | tf_op jit(solution)/shard_map/ppermute | solution.py:184
  406.4 6.2 %copy-start.7 = (f32[256,256]{1,0:T(8,128)}, f32[256,256]{1,0:T(8,128)S(1)}, u32[]{:S(2)}) copy-start(f32[256,256]{1,0:T(8,128)S(1)} %fusion.24) | copy-start | bytes 786436
  406.7 6.0 %copy-start.8 = (f32[256,256]{1,0:T(8,128)}, f32[256,256]{1,0:T(8,128)S(1)}, u32[]{:S(2)}) copy-start(f32[256,256]{1,0:T(8,128)S(1)} %fusion.4) | copy-start | bytes 786436
  (5 other events, 8.2 us)
Sparse Core Ops, SparseCore 0:
  10.4 136.6 all-gather.2
  149.5 43.8 all-gather.4

commit v2 on v1

--- a/solution.py
+++ b/solution.py
@@ -146,10 +146,13 @@
     )(row_flags, col_flags, inverse, panel)
 
 
-def column_rows(panel):
+def routed(panel):
     n_row, n_col = lax.axis_size("row"), lax.axis_size("col")
     routes = [(k, k % n_row * n_col + k // n_row) for k in range(n_row * n_col)]
-    moved = lax.ppermute(panel, BOTH, routes)
+    return lax.ppermute(panel, BOTH, routes)
+
+
+def gathered(moved):
     return lax.all_gather(moved, "row", axis=0, tiled=True)
 
 
@@ -159,17 +162,19 @@
     index = lax.axis_index("col")
     chip, core = index // 2, index % 2
     step = 1 - 2 * core
-    parts = partial.reshape(chips, 2, rows_here, partial.shape[1])
-    theirs = lax.dynamic_index_in_dim(parts, 1 - core, 1, keepdims=False)
-    mine = lax.dynamic_index_in_dim(parts, core, 1, keepdims=False)
-    got = lax.ppermute(theirs, "col", [(k, k ^ 1) for k in range(n_col)])
+    swap = [(k, k ^ 1) for k in range(n_col)]
     ring = [((2 * z + c), (z + 1 - 2 * c) % chips * 2 + c) for z in range(chips) for c in (0, 1)]
 
+    def part(place, side):
+        start = (lax.rem(place + 2 * chips, chips) * 2 + side) * rows_here
+        return lax.dynamic_slice_in_dim(partial, start, rows_here, 0)
+
+    got = []
+    for s in range(chips):
+        got.append(lax.ppermute(part(chip + step * ((s + 1) % chips), 1 - core), "col", swap))
+
     def term(s):
-        place = (chip - step * (s + 1) + 2 * chips * (s + 1)) % chips
-        return lax.dynamic_index_in_dim(mine, place, 0, keepdims=False) + (
-            lax.dynamic_index_in_dim(got, place, 0, keepdims=False)
-        )
+        return part(chip - step * ((s + 1) % chips), core) + got[s]
 
     running = term(0)
     for s in range(1, chips):
@@ -177,13 +182,96 @@
     return running
 
 
+def sum_kernel(value, out, got_col, got_row, middle, sent_col, came_col, sent_row, came_row):
+    n_col, n_row = value.shape[0], value.shape[1]
+    row, col = lax.axis_index("row"), lax.axis_index("col")
+    mesh_ids = pl.DeviceIdType.MESH
+
+    barrier = pltpu.get_barrier_semaphore()
+    for k in range(1, n_col):
+        pl.semaphore_signal(
+            barrier, inc=1, device_id=(row, lax.rem(col + k, n_col)), device_id_type=mesh_ids
+        )
+    for k in range(1, n_row):
+        pl.semaphore_signal(
+            barrier, inc=1, device_id=(lax.rem(row + k, n_row), col), device_id_type=mesh_ids
+        )
+    pl.semaphore_wait(barrier, n_col + n_row - 2)
+
+    def along_col(phase, source, target):
+        copies = []
+        for k in range(1, n_col):
+            there = lax.rem(col + k, n_col)
+            copies.append(
+                pltpu.make_async_remote_copy(
+                    src_ref=source(there),
+                    dst_ref=target(k),
+                    send_sem=sent_col.at[phase, k],
+                    recv_sem=came_col.at[phase, k],
+                    device_id=(row, there),
+                    device_id_type=mesh_ids,
+                )
+            )
+        for copy in copies:
+            copy.start()
+        for copy in copies:
+            copy.wait()
+
+    def along_row(phase, source, target):
+        copies = []
+        for k in range(1, n_row):
+            there = lax.rem(row + k, n_row)
+            copies.append(
+                pltpu.make_async_remote_copy(
+                    src_ref=source(there),
+                    dst_ref=target(k),
+                    send_sem=sent_row.at[phase, k],
+                    recv_sem=came_row.at[phase, k],
+                    device_id=(there, col),
+                    device_id_type=mesh_ids,
+                )
+            )
+        for copy in copies:
+            copy.start()
+        for copy in copies:
+            copy.wait()
+
+    along_col(0, lambda there: value.at[there], lambda k: got_col.at[k])
+    summed = value[col]
+    for k in range(1, n_col):
+        summed += got_col[k]
+    middle[...] = summed
+    along_row(0, lambda there: middle.at[there], lambda k: got_row.at[k])
+    final = middle[row]
+    for k in range(1, n_row):
+        final += got_row[k]
+    out[col, row] = final
+    along_row(1, lambda there: out.at[col, row], lambda k: out.at[col, row])
+    along_col(1, lambda there: out.at[col], lambda k: out.at[col])
+
+
 def total_of(value):
-    devices = lax.axis_size("row") * lax.axis_size("col")
-    bit = 1
-    while bit < devices:
-        value = value + lax.ppermute(value, BOTH, [(k, k ^ bit) for k in range(devices)])
-        bit *= 2
-    return value
+    n_row, n_col = lax.axis_size("row"), lax.axis_size("col")
+    across = value.shape[-1]
+    each = value.size // (n_row * n_col * across)
+    shape = (n_col, n_row, each, across)
+    summed = pl.pallas_call(
+        sum_kernel,
+        out_shape=jax.ShapeDtypeStruct(shape, jnp.float32),
+        in_specs=[pl.BlockSpec(memory_space=pltpu.VMEM)],
+        out_specs=pl.BlockSpec(memory_space=pltpu.VMEM),
+        scratch_shapes=[
+            pltpu.VMEM(shape, jnp.float32),
+            pltpu.VMEM(shape[1:], jnp.float32),
+            pltpu.VMEM(shape[1:], jnp.float32),
+            pltpu.SemaphoreType.DMA((2, n_col)),
+            pltpu.SemaphoreType.DMA((2, n_col)),
+            pltpu.SemaphoreType.DMA((2, n_row)),
+            pltpu.SemaphoreType.DMA((2, n_row)),
+        ],
+        compiler_params=pltpu.CompilerParams(collective_id=0, has_side_effects=True),
+    )(value.reshape(shape))
+    return summed.reshape(value.shape)
 
 
 def per_device(
@@ -201,8 +289,10 @@
     child_mask = local_mask(child_blocks, rows_here)
     parent_masked = jnp.where(parent_mask, parent_panel, 0)
     child_masked = jnp.where(child_mask, child_panel, 0)
-    parent_rows = column_rows(parent_panel)
-    child_rows = column_rows(child_panel)
+    parent_moved = routed(parent_panel)
+    parent_moved, child_panel_later = lax.optimization_barrier((parent_moved, child_panel))
+    parent_rows = gathered(parent_moved)
+    child_rows = gathered(routed(child_panel_later))
     parent_partial = product(inverse, parent_rows, parent_blocks)
     child_partial = product(inverse, child_rows, child_blocks)
     parent_column = jnp.where(parent_mask, -summed_rows(parent_partial, rows_here), 0)
@@ -212,9 +302,8 @@
     carried = matmul(parent_column, child_top)
     child_column = jnp.where(child_mask, -(carried + child_image), 0)
     image_local = matmul(child_masked.T, child_image)
-    first_sums = total_of(jnp.stack([parent_local, cross_local]))
-    parent_sum, cross_sum = first_sums[0], first_sums[1]
-    image_sum = total_of(image_local)
+    sums = total_of(jnp.stack([parent_local, cross_local, image_local]))
+    parent_sum, cross_sum, image_sum = sums[0], sums[1], sums[2]
     parent_diagonal = diag_parent - parent_sum
     child_upper = -(matmul(parent_diagonal, child_top) + cross_sum)
     child_diagonal = (

time: 414 us -> 388 us (0.937); the launches traced: 419 us -> 385 us
  waiting for transfers between devices: 268 us -> 217 us
  Pallas kernels: 67.8 us -> 89.9 us
  starting transfers between devices: 33.7 us -> 16.7 us
  matrix products: 5.22 us -> 12.8 us
    pallas_call x0 -> x1, Pallas kernels: none -> 47.7 us  [total_of(): pl.pallas_call(sum_kernel, out_shape=jax.ShapeDtypeStruct(shape, jnp.floa...]
    ppermute x14 -> x10, waiting for transfers between devices: 35.9 us -> 0.03 us  [the longest x8 0.02 us: summed_rows(): lax.ppermute(part(chip + step * ((s + 1) % chips), 1 - core), 'col', swap)]
    pallas_call x2, Pallas kernels: 67.8 us -> 42.2 us  [product(): pl.pallas_call(product_kernel, out_shape=jax.ShapeDtypeStruct((height, ac...]
    ppermute x14 -> x10, starting transfers between devices: 32.8 us -> 13 us  [the longest x8 9.26 us: summed_rows(): lax.ppermute(part(chip + step * ((s + 1) % chips), 1 - core), 'col', swap)]
    ppermute x6, waiting for transfers between devices: 99.1 us -> 80 us  [summed_rows(): running = lax.ppermute(running, 'col', ring) + term(s)]
    dot_general x7, matrix products: 5.22 us -> 12.8 us  [matmul(): jnp.dot(left, right, precision=lax.Precision.HIGH, preferred_element_type...]
    all_gather x2, waiting for transfers between devices: 133 us -> 137 us  [gathered(): return lax.all_gather(moved, 'row', axis=0, tiled=True)]
    unnamed x32 -> x28, local copies, waits for them, and re-layouts: 11.6 us -> 11.7 us
  transfers between devices with their start and end apart: 22 -> 18, of which waited for: 15 -> 8; matrix products, arithmetic and copies ran while one was open for 6% -> 6% of each run, Pallas kernels for 16% -> 11%
where the time goes in v2:
time: 388 us; the launch traced here: 385 us
  waiting for transfers between devices  217 us (56%)
  Pallas kernels  89.9 us (23%)
  local copies, waits for them, and re-layouts  18.7 us (5%)
  starting transfers between devices  16.7 us (4%)
  other arithmetic  15.4 us (4%)
  between operations  14.4 us (4%)
  matrix products  12.8 us (3%)
    all_gather x2, waiting for transfers between devices, gathered(): return lax.all_gather(moved, 'row', axis=0, tiled=True)  137 us
    ppermute x6, waiting for transfers between devices, summed_rows(): running = lax.ppermute(running, 'col', ring) + term(s)  80 us
    pallas_call x1, Pallas kernels, total_of(): pl.pallas_call(sum_kernel, out_shape=jax.ShapeDtypeStruct(shape, jnp.floa...  47.7 us
    pallas_call x2, Pallas kernels, product(): pl.pallas_call(product_kernel, out_shape=jax.ShapeDtypeStruct((height, ac...  42.2 us
    dot_general x7, matrix products, matmul(): jnp.dot(left, right, precision=lax.Precision.HIGH, preferred_element_type...  12.8 us
    unnamed x28, local copies, waits for them, and re-layouts  11.7 us
    ppermute x8, starting transfers between devices, summed_rows(): lax.ppermute(part(chip + step * ((s + 1) % chips), 1 - core), 'col', swap)  9.26 us
    add x4, other arithmetic, summed_rows(): running = lax.ppermute(running, 'col', ring) + term(s)  8.26 us
  transfers between devices with their start and end apart: 18, of which 8 were waited for; matrix products, arithmetic and copies ran while one was open for 6% of the time, Pallas kernels for 11%

profile of v2, /device:TPU:0, one launch (start us, length us, event | category | flops | bytes accessed | tf_op | source)
XLA Modules:
  0.0 385.0 jit_solution(1078013955256418789)
XLA Ops:
  7.2 1.9 collective-permute-start
  10.1 1.8 collective-permute-start.8
  16.0 131.1 %all-gather.3.cloned.1.call-done.panel = f32[3072,256]{1,0:T(8,128)} async-done(((f32[768,256]{1,0:T(8,128)}), f32[3072,256]{1,0:T(8,128)}) %all-gather.3.cloned.1.call-update) | async-done | bytes 3145744 | tf_op jit(solution)/shard_map/all_gather | solution.py:156
  147.1 1.9 copy-done.3
  148.9 33.8 %shard_map.119 = f32[6144,256]{1,0:T(8,128)S(1)} custom-call(s32[48]{0:T(128)S(1)} %dynamic_slice.67.row_flags, s32[24]{0:T(128)S(1)} %dynamic_slice.68.col_flags, f32[6144,3072]{1,0:T(8,128)} %inverse.3, f32[3072,256]{1,0:T(8,128)S(1)} %copy-done.3), custom_call_target="tpu_custom_call" | custom-call | flops 14495514624 | bytes 37748736 | tf_op jit(solution)/shard_map/pallas_call | solution.py:122
  182.8 2.6 copy-done.2
  185.4 1.4 constant_dynamic-slice_fusion.4
  186.8 5.9 %all-gather.5.cloned.1.call-done.panel = f32[3072,256]{1,0:T(8,128)} async-done(((f32[768,256]{1,0:T(8,128)}), f32[3072,256]{1,0:T(8,128)}) %all-gather.5.cloned.1.call-update) | async-done | bytes 3145744 | tf_op jit(solution)/shard_map/all_gather | solution.py:156
  192.8 1.9 copy-done.4
  194.7 8.4 %shard_map.120 = f32[6144,256]{1,0:T(8,128)S(1)} custom-call(s32[48]{0:T(128)S(1)} %dynamic_slice.78.row_flags, s32[24]{0:T(128)S(1)} %dynamic_slice.79.col_flags, f32[6144,3072]{1,0:T(8,128)} %inverse.3, f32[3072,256]{1,0:T(8,128)S(1)} %copy-done.4), custom_call_target="tpu_custom_call" | custom-call | flops 14495514624 | bytes 37748736 | tf_op jit(solution)/shard_map/pallas_call | solution.py:122
  203.1 2.6 copy-done.1
  205.7 1.7 constant_dynamic-slice_fusion
  209.2 3.5 collective-permute-start.2
  212.7 3.8 collective-permute-start.5
  217.9 17.4 %collective-permute-done.2 = f32[768,256]{1,0:T(8,128)S(1)} collective-permute-done((f32[768,256]{1,0:T(8,128)S(1)}, f32[768,256]{1,0:T(8,128)S(1)}, u32[]{:S(2)}, u32[]{:S(2)}) %collective-permute-start.2) | collective-permute-done | bytes 786464 | tf_op jit(solution)/shard_map/ppermute | solution.py:181
  235.2 1.5 add_add_fusion.3
  236.9 2.4 collective-permute-start.7
  239.4 12.6 %collective-permute-done.10 = f32[768,256]{1,0:T(8,128)S(1)} collective-permute-done((f32[768,256]{1,0:T(8,128)S(1)}, f32[768,256]{1,0:T(8,128)S(1)}, u32[]{:S(2)}, u32[]{:S(2)}) %collective-permute-start.10) | collective-permute-done | bytes 786464 | tf_op jit(solution)/shard_map/ppermute | solution.py:181
  252.1 2.2 add_add_fusion.1
  254.2 14.7 %collective-permute-done.4 = f32[768,256]{1,0:T(8,128)S(1)} collective-permute-done((f32[768,256]{1,0:T(8,128)S(1)}, f32[768,256]{1,0:T(8,128)S(1)}, u32[]{:S(2)}, u32[]{:S(2)}) %collective-permute-start.4) | collective-permute-done | bytes 786464 | tf_op jit(solution)/shard_map/ppermute | solution.py:181
  268.9 2.2 add_add_fusion.2
  271.8 2.4 collective-permute-start.15
  274.2 11.7 %collective-permute-done.12 = f32[768,256]{1,0:T(8,128)} collective-permute-done((f32[768,256]{1,0:T(8,128)}, f32[768,256]{1,0:T(8,128)}, u32[]{:S(2)}, u32[]{:S(2)}) %collective-permute-start.12) | collective-permute-done | bytes 786464 | tf_op jit(solution)/shard_map/ppermute | solution.py:181
  285.9 2.4 add_add_fusion
  290.0 12.7 %collective-permute-done.6 = f32[768,256]{1,0:T(8,128)} collective-permute-done((f32[768,256]{1,0:T(8,128)}, f32[768,256]{1,0:T(8,128)}, u32[]{:S(2)}, u32[]{:S(2)}) %collective-permute-start.6) | collective-permute-done | bytes 786464 | tf_op jit(solution)/shard_map/ppermute | solution.py:181
  302.7 1.8 negate_select_fusion
  304.5 2.3 convolution_bitcast_fusion.3
  307.8 11.0 %collective-permute-done.14 = f32[768,256]{1,0:T(8,128)S(1)} collective-permute-done((f32[768,256]{1,0:T(8,128)}, f32[768,256]{1,0:T(8,128)S(1)}, u32[]{:S(2)}, u32[]{:S(2)}) %collective-permute-start.14) | collective-permute-done | bytes 786464 | tf_op jit(solution)/shard_map/ppermute | solution.py:181
  318.8 2.2 convolution_bitcast_fusion.1
  321.9 47.7 %shard_map.121 = f32[8,4,24,256]{3,2,1,0:T(8,128)} custom-call(f32[8,4,24,256]{3,2,1,0:T(8,128)} %bitcast.38), custom_call_target="tpu_custom_call" | custom-call | tf_op jit(solution)/shard_map/pallas_call | solution.py:258
  373.5 2.1 fusion.2
  375.6 2.5 fusion.1
  (63 shorter events, 16.4 us)
Async XLA Ops:
  7.2 363.5 %copy-start = (f32[256,256]{1,0:T(8,128)S(1)}, f32[256,256]{1,0:T(8,128)}, u32[]{:S(2)}) copy-start(f32[256,256]{1,0:T(8,128)} %param.11) | copy-start | bytes 786436
  7.2 139.9 %all-gather.3.cloned.1.call-start = ((), (), s32[]{:S(2)}) async-start(), calls=%async_computation | async-start | bytes 3932160 | tf_op jit(solution)/shard_map/all_gather | solution.py:156
  7.2 1.9 collective-permute-start
  9.2 0.9 copy-start.9
  10.1 182.7 %all-gather.5.cloned.1.call-start = ((), (), s32[]{:S(2)}) async-start(), calls=%async_computation.1 | async-start | bytes 3932160 | tf_op jit(solution)/shard_map/all_gather | solution.py:156
  10.1 1.8 collective-permute-start.8
  11.9 0.9 copy-start.10
  147.1 1.9 copy-start.3
  182.8 2.6 copy-start.2
  186.8 21.1 %collective-permute-start.1 = (f32[768,256]{1,0:T(8,128)S(1)}, f32[768,256]{1,0:T(8,128)S(1)}, u32[]{:S(2)}, u32[]{:S(2)}) collective-permute-start(f32[768,256]{1,0:T(8,128)S(1)} %get-tuple-element.16), channel_id=1, source_target_pairs={{0,1},{1,0},{2,3},{3,2},{4,5},{5,4},{6,7},{7,6},{8,9},{9,8},{10,11... | collective-permute-start | bytes 2359304 | tf_op jit(solution)/shard_map/ppermute | solution.py:174
  192.8 1.9 copy-start.4
  203.0 2.6 copy-start.1
  205.7 31.1 %copy-start.12 = (s32[192]{0:T(256)S(1)}, s32[192]{0:T(256)}, u32[]{:S(2)}) copy-start(s32[192]{0:T(256)} %param.14) | copy-start | bytes 2308
  207.4 9.1 %collective-permute-start.9 = (f32[768,256]{1,0:T(8,128)}, f32[768,256]{1,0:T(8,128)S(1)}, u32[]{:S(2)}, u32[]{:S(2)}) collective-permute-start(f32[768,256]{1,0:T(8,128)} %get-tuple-element.12), channel_id=1, source_target_pairs={{0,1},{1,0},{2,3},{3,2},{4,5},{5,4},{6,7},{7,6},{8,9},{9,8},{10,11... | collective-permute-start | bytes 2359304 | tf_op jit(solution)/shard_map/ppermute | solution.py:174
  207.9 9.9 %collective-permute-start.3 = (f32[768,256]{1,0:T(8,128)S(1)}, f32[768,256]{1,0:T(8,128)}, u32[]{:S(2)}, u32[]{:S(2)}) collective-permute-start(f32[768,256]{1,0:T(8,128)S(1)} %get-tuple-element.15), channel_id=1, source_target_pairs={{0,1},{1,0},{2,3},{3,2},{4,5},{5,4},{6,7},{7,6},{8,9},{9,8},{10,11... | collective-permute-start | bytes 2359304 | tf_op jit(solution)/shard_map/ppermute | solution.py:174
  209.2 61.9 %copy-start.13 = (s32[192]{0:T(256)S(1)}, s32[192]{0:T(256)}, u32[]{:S(2)}) copy-start(s32[192]{0:T(256)} %param.15) | copy-start | bytes 2308
  209.2 26.0 %collective-permute-start.2 = (f32[768,256]{1,0:T(8,128)S(1)}, f32[768,256]{1,0:T(8,128)S(1)}, u32[]{:S(2)}, u32[]{:S(2)}) collective-permute-start(f32[768,256]{1,0:T(8,128)S(1)} %dynamic-slice_add_fusion.1), channel_id=1, source_target_pairs={{0,2},{1,7},{2,4},{3,1},{4,6},{5,3},{6,0},{7,5},{8,10},{9,15},{10,... | collective-permute-start | bytes 2359304 | tf_op jit(solution)/shard_map/ppermute | solution.py:181
  212.7 41.5 %collective-permute-start.5 = (f32[768,256]{1,0:T(8,128)}, f32[768,256]{1,0:T(8,128)S(1)}, u32[]{:S(2)}, u32[]{:S(2)}) collective-permute-start(f32[768,256]{1,0:T(8,128)} %get-tuple-element.14), channel_id=1, source_target_pairs={{0,1},{1,0},{2,3},{3,2},{4,5},{5,4},{6,7},{7,6},{8,9},{9,8},{10,11... | collective-permute-start | bytes 2359304 | tf_op jit(solution)/shard_map/ppermute | solution.py:174
  216.5 22.8 %collective-permute-start.11 = (f32[768,256]{1,0:T(8,128)}, f32[768,256]{1,0:T(8,128)S(1)}, u32[]{:S(2)}, u32[]{:S(2)}) collective-permute-start(f32[768,256]{1,0:T(8,128)} %get-tuple-element.11), channel_id=1, source_target_pairs={{0,1},{1,0},{2,3},{3,2},{4,5},{5,4},{6,7},{7,6},{8,9},{9,8},{10,11... | collective-permute-start | bytes 2359304 | tf_op jit(solution)/shard_map/ppermute | solution.py:174
  217.8 34.3 %collective-permute-start.10 = (f32[768,256]{1,0:T(8,128)S(1)}, f32[768,256]{1,0:T(8,128)S(1)}, u32[]{:S(2)}, u32[]{:S(2)}) collective-permute-start(f32[768,256]{1,0:T(8,128)S(1)} %dynamic-slice_add_fusion), channel_id=1, source_target_pairs={{0,2},{1,7},{2,4},{3,1},{4,6},{5,3},{6,0},{7,5},{8,10},{9,15},{10,... | collective-permute-start | bytes 2359304 | tf_op jit(solution)/shard_map/ppermute | solution.py:181
  236.7 32.2 %collective-permute-start.4 = (f32[768,256]{1,0:T(8,128)S(1)}, f32[768,256]{1,0:T(8,128)S(1)}, u32[]{:S(2)}, u32[]{:S(2)}) collective-permute-start(f32[768,256]{1,0:T(8,128)S(1)} %add_add_fusion.3), channel_id=1, source_target_pairs={{0,2},{1,7},{2,4},{3,1},{4,6},{5,3},{6,0},{7,5},{8,10},{9,15},{10,... | collective-permute-start | bytes 2359304 | tf_op jit(solution)/shard_map/ppermute | solution.py:181
  236.9 52.2 %collective-permute-start.7 = (f32[768,256]{1,0:T(8,128)}, f32[768,256]{1,0:T(8,128)S(1)}, u32[]{:S(2)}, u32[]{:S(2)}) collective-permute-start(f32[768,256]{1,0:T(8,128)} %get-tuple-element.13), channel_id=1, source_target_pairs={{0,1},{1,0},{2,3},{3,2},{4,5},{5,4},{6,7},{7,6},{8,9},{9,8},{10,11... | collective-permute-start | bytes 2359304 | tf_op jit(solution)/shard_map/ppermute | solution.py:174
  239.3 34.9 %collective-permute-start.13 = (f32[768,256]{1,0:T(8,128)}, f32[768,256]{1,0:T(8,128)S(1)}, u32[]{:S(2)}, u32[]{:S(2)}) collective-permute-start(f32[768,256]{1,0:T(8,128)} %get-tuple-element.10), channel_id=1, source_target_pairs={{0,1},{1,0},{2,3},{3,2},{4,5},{5,4},{6,7},{7,6},{8,9},{9,8},{10,11... | collective-permute-start | bytes 2359304 | tf_op jit(solution)/shard_map/ppermute | solution.py:174
  254.2 52.6 %copy-start.6 = (f32[768,256]{1,0:T(8,128)S(1)}, f32[768,256]{1,0:T(8,128)}, u32[]{:S(2)}) copy-start(f32[768,256]{1,0:T(8,128)} %param.10) | copy-start | bytes 2359300
  254.2 31.6 %collective-permute-start.12 = (f32[768,256]{1,0:T(8,128)}, f32[768,256]{1,0:T(8,128)}, u32[]{:S(2)}, u32[]{:S(2)}) collective-permute-start(f32[768,256]{1,0:T(8,128)} %add_add_fusion.1), channel_id=1, source_target_pairs={{0,2},{1,7},{2,4},{3,1},{4,6},{5,3},{6,0},{7,5},{8,10},{9,15},{10,... | collective-permute-start | bytes 2359304 | tf_op jit(solution)/shard_map/ppermute | solution.py:181
  271.1 31.6 %collective-permute-start.6 = (f32[768,256]{1,0:T(8,128)}, f32[768,256]{1,0:T(8,128)}, u32[]{:S(2)}, u32[]{:S(2)}) collective-permute-start(f32[768,256]{1,0:T(8,128)} %add_add_fusion.2), channel_id=1, source_target_pairs={{0,2},{1,7},{2,4},{3,1},{4,6},{5,3},{6,0},{7,5},{8,10},{9,15},{10,... | collective-permute-start | bytes 2359304 | tf_op jit(solution)/shard_map/ppermute | solution.py:181
  271.8 36.0 %collective-permute-start.15 = (f32[768,256]{1,0:T(8,128)}, f32[768,256]{1,0:T(8,128)S(1)}, u32[]{:S(2)}, u32[]{:S(2)}) collective-permute-start(f32[768,256]{1,0:T(8,128)} %get-tuple-element.9), channel_id=1, source_target_pairs={{0,1},{1,0},{2,3},{3,2},{4,5},{5,4},{6,7},{7,6},{8,9},{9,8},{10,11... | collective-permute-start | bytes 2359304 | tf_op jit(solution)/shard_map/ppermute | solution.py:174
  288.3 30.5 %collective-permute-start.14 = (f32[768,256]{1,0:T(8,128)}, f32[768,256]{1,0:T(8,128)S(1)}, u32[]{:S(2)}, u32[]{:S(2)}) collective-permute-start(f32[768,256]{1,0:T(8,128)} %add_add_fusion), channel_id=1, source_target_pairs={{0,2},{1,7},{2,4},{3,1},{4,6},{5,3},{6,0},{7,5},{8,10},{9,15},{10,... | collective-permute-start | bytes 2359304 | tf_op jit(solution)/shard_map/ppermute | solution.py:181
  289.1 0.9 copy-start.11
  304.5 71.1 %copy-start.5 = (f32[768,256]{1,0:T(8,128)}, f32[768,256]{1,0:T(8,128)S(1)}, u32[]{:S(2)}) copy-start(f32[768,256]{1,0:T(8,128)S(1)} %negate_select_fusion) | copy-start | bytes 2359300
  370.7 7.5 %copy-start.7 = (f32[256,256]{1,0:T(8,128)}, f32[256,256]{1,0:T(8,128)S(1)}, u32[]{:S(2)}) copy-start(f32[256,256]{1,0:T(8,128)S(1)} %fusion.14) | copy-start | bytes 786436
  372.0 6.1 %copy-start.8 = (f32[256,256]{1,0:T(8,128)}, f32[256,256]{1,0:T(8,128)S(1)}, u32[]{:S(2)}) copy-start(f32[256,256]{1,0:T(8,128)S(1)} %fusion.4) | copy-start | bytes 786436
Sparse Core Ops, SparseCore 0:
  10.4 136.6 all-gather.2
  148.9 43.8 all-gather.4

commit v3 on v2

--- a/solution.py
+++ b/solution.py
@@ -148,12 +148,32 @@
 
 def routed(panel):
     n_row, n_col = lax.axis_size("row"), lax.axis_size("col")
-    routes = [(k, k % n_row * n_col + k // n_row) for k in range(n_row * n_col)]
-    return lax.ppermute(panel, BOTH, routes)
+    row, col = lax.axis_index("row"), lax.axis_index("col")
+    ratio = n_col // n_row
+    piece = panel.shape[0] // n_row
+
+    def pick(pieces, place):
+        return lax.dynamic_slice_in_dim(pieces, lax.rem(place + n_row, n_row) * piece, piece, 0)
+
+    across = [pick(panel, row)]
+    for k in range(1, n_row):
+        lanes = [(r, (r + k) % n_row) for r in range(n_row)]
+        across.append(lax.ppermute(pick(panel, row + k), "row", lanes))
+    across = jnp.concatenate(across, axis=0)
+    along = []
+    for m in range(n_row):
+        source = lax.rem(col + m, n_row)
+        lanes = [(c, ratio * ((c + m) % n_row) + c // n_row) for c in range(n_col)]
+        along.append(lax.ppermute(pick(across, row - source), "col", lanes))
+    along = jnp.concatenate(along, axis=0)
+    return jnp.concatenate([pick(along, col // ratio - j) for j in range(n_row)], axis=0)
 
 
 def gathered(moved):
-    return lax.all_gather(moved, "row", axis=0, tiled=True)
+    n_row = lax.axis_size("row")
+    rows = lax.all_gather(moved, "row", axis=0, tiled=True)
+    pieces = rows.reshape(n_row, n_row, moved.shape[0] // n_row, moved.shape[1])
+    return pieces.transpose(1, 0, 2, 3).reshape(rows.shape)
 
 
 def summed_rows(partial, rows_here):
@@ -182,8 +202,8 @@
     return running
 
 
-def sum_kernel(value, out, got_col, got_row, middle, sent_col, came_col, sent_row, came_row):
-    n_col, n_row = value.shape[0], value.shape[1]
+def sum_kernel(value, out, got_row, got_col, middle, sent_col, came_col, sent_row, came_row):
+    n_row, n_col = value.shape[0], value.shape[1]
     row, col = lax.axis_index("row"), lax.axis_index("col")
     mesh_ids = pl.DeviceIdType.MESH
 
@@ -236,25 +256,25 @@
         for copy in copies:
             copy.wait()
 
-    along_col(0, lambda there: value.at[there], lambda k: got_col.at[k])
-    summed = value[col]
+    along_row(0, lambda there: value.at[there], lambda k: got_row.at[k])
+    summed = value[row]
+    for k in range(1, n_row):
+        summed += got_row[k]
+    middle[...] = summed
+    along_col(0, lambda there: middle.at[there], lambda k: got_col.at[k])
+    final = middle[col]
     for k in range(1, n_col):
-        summed += got_col[k]
-    middle[...] = summed
-    along_row(0, lambda there: middle.at[there], lambda k: got_row.at[k])
-    final = middle[row]
-    for k in range(1, n_row):
-        final += got_row[k]
-    out[col, row] = final
-    along_row(1, lambda there: out.at[col, row], lambda k: out.at[col, row])
-    along_col(1, lambda there: out.at[col], lambda k: out.at[col])
+        final += got_col[k]
+    out[row, col] = final
+    along_col(1, lambda there: out.at[row, col], lambda k: out.at[row, col])
+    along_row(1, lambda there: out.at[row], lambda k: out.at[row])
 
 
 def total_of(value):
     n_row, n_col = lax.axis_size("row"), lax.axis_size("col")
     across = value.shape[-1]
     each = value.size // (n_row * n_col * across)
-    shape = (n_col, n_row, each, across)
+    shape = (n_row, n_col, each, across)
     summed = pl.pallas_call(
         sum_kernel,
         out_shape=jax.ShapeDtypeStruct(shape, jnp.float32),

time: 388 us -> 325 us (0.84); the launches traced: 385 us -> 327 us
  waiting for transfers between devices: 217 us -> 122 us
  starting transfers between devices: 16.7 us -> 53.6 us
    all_gather x2, waiting for transfers between devices: 137 us -> 13.6 us  [gathered(): rows = lax.all_gather(moved, 'row', axis=0, tiled=True)]
    ppermute x2 -> x14, starting transfers between devices: 3.72 us -> 36.5 us  [the longest x8 28.9 us: routed(): along.append(lax.ppermute(pick(across, row - source), 'col', lanes))]
    ppermute x2 -> x14, waiting for transfers between devices: 0.01 us -> 27.6 us  [the longest x6 16.5 us: routed(): across.append(lax.ppermute(pick(panel, row + k), 'row', lanes))]
    pallas_call x2, Pallas kernels: 42.2 us -> 56.8 us  [product(): pl.pallas_call(product_kernel, out_shape=jax.ShapeDtypeStruct((height, ac...]
    pallas_call x1, Pallas kernels: 47.7 us -> 35.4 us  [total_of(): pl.pallas_call(sum_kernel, out_shape=jax.ShapeDtypeStruct(shape, jnp.floa...]
    unnamed x28 -> x30, local copies, waits for them, and re-layouts: 11.7 us -> 6.39 us
    reshape x0 -> x2, local copies, waits for them, and re-layouts: none -> 4.32 us  [gathered(): pieces = rows.reshape(n_row, n_row, moved.shape[0] // n_row, moved.shape[1])]
  transfers between devices with their start and end apart: 18 -> 30, of which waited for: 8 -> 16; matrix products, arithmetic and copies ran while one was open for 6% -> 8% of each run, Pallas kernels for 11% -> 17%
where the time goes in v3:
time: 325 us; the launch traced here: 327 us
  waiting for transfers between devices  122 us (38%)
  Pallas kernels  92.2 us (28%)
  starting transfers between devices  53.6 us (16%)
  other arithmetic  17.6 us (5%)
  local copies, waits for them, and re-layouts  16.7 us (5%)
  between operations  14.7 us (5%)
  matrix products  10.8 us (3%)
    ppermute x6, waiting for transfers between devices, summed_rows(): running = lax.ppermute(running, 'col', ring) + term(s)  80.2 us
    pallas_call x2, Pallas kernels, product(): pl.pallas_call(product_kernel, out_shape=jax.ShapeDtypeStruct((height, ac...  56.8 us
    pallas_call x1, Pallas kernels, total_of(): pl.pallas_call(sum_kernel, out_shape=jax.ShapeDtypeStruct(shape, jnp.floa...  35.4 us
    ppermute x8, starting transfers between devices, routed(): along.append(lax.ppermute(pick(across, row - source), 'col', lanes))  28.9 us
    ppermute x6, waiting for transfers between devices, routed(): across.append(lax.ppermute(pick(panel, row + k), 'row', lanes))  16.5 us
    all_gather x2, waiting for transfers between devices, gathered(): rows = lax.all_gather(moved, 'row', axis=0, tiled=True)  13.6 us
    ppermute x8, starting transfers between devices, summed_rows(): lax.ppermute(part(chip + step * ((s + 1) % chips), 1 - core), 'col', swap)  11.5 us
    ppermute x8, waiting for transfers between devices, routed(): along.append(lax.ppermute(pick(across, row - source), 'col', lanes))  11.2 us
  transfers between devices with their start and end apart: 30, of which 16 were waited for; matrix products, arithmetic and copies ran while one was open for 8% of the time, Pallas kernels for 17%

profile of v3, /device:TPU:0, one launch (start us, length us, event | category | flops | bytes accessed | tf_op | source)
XLA Modules:
  0.0 327.1 jit_solution(675653788116287038)
XLA Ops:
  8.6 4.0 %collective-permute-start.2 = (f32[192,256]{1,0:T(8,128)S(1)}, f32[192,256]{1,0:T(8,128)S(1)}, u32[]{:S(2)}, u32[]{:S(2)}) collective-permute-start(f32[192,256]{1,0:T(8,128)S(1)} %get-tuple-element.40), channel_id=1, source_target_pairs={{0,24},{8,0},{16,8},{24,16},{1,25},{9,1},{17,9},{25,17},{2,26},{10... | collective-permute-start | bytes 589832 | tf_op jit(solution)/shard_map/ppermute | solution.py:161
  13.7 4.2 %collective-permute-done.2 = f32[192,256]{1,0:T(8,128)S(1)} collective-permute-done((f32[192,256]{1,0:T(8,128)S(1)}, f32[192,256]{1,0:T(8,128)S(1)}, u32[]{:S(2)}, u32[]{:S(2)}) %collective-permute-start.2) | collective-permute-done | bytes 196640 | tf_op jit(solution)/shard_map/ppermute | solution.py:161
  17.9 5.3 %collective-permute-done.1 = f32[192,256]{1,0:T(8,128)S(1)} collective-permute-done((f32[192,256]{1,0:T(8,128)S(1)}, f32[192,256]{1,0:T(8,128)S(1)}, u32[]{:S(2)}, u32[]{:S(2)}) %collective-permute-start.1) | collective-permute-done | bytes 196640 | tf_op jit(solution)/shard_map/ppermute | solution.py:161
  24.0 6.3 %collective-permute-start.4 = (f32[192,256]{1,0:T(8,128)S(1)}, f32[192,256]{1,0:T(8,128)S(1)}, u32[]{:S(2)}, u32[]{:S(2)}) collective-permute-start(f32[192,256]{1,0:T(8,128)S(1)} %get-tuple-element.35), channel_id=1, source_target_pairs={{0,2},{1,4},{2,6},{3,0},{4,3},{5,5},{6,7},{7,1},{8,10},{9,12},{10,... | collective-permute-start | bytes 589832 | tf_op jit(solution)/shard_map/ppermute | solution.py:167
  30.4 2.3 collective-permute-start.5
  32.6 2.7 collective-permute-start.6
  35.4 4.3 %collective-permute-done.4 = f32[192,256]{1,0:T(8,128)S(1)} collective-permute-done((f32[192,256]{1,0:T(8,128)S(1)}, f32[192,256]{1,0:T(8,128)S(1)}, u32[]{:S(2)}, u32[]{:S(2)}) %collective-permute-start.4) | collective-permute-done | bytes 196640 | tf_op jit(solution)/shard_map/ppermute | solution.py:167
  44.7 3.1 collective-permute-done.16
  52.6 10.8 %collective-permute-start.18 = (f32[192,256]{1,0:T(8,128)S(1)}, f32[192,256]{1,0:T(8,128)S(1)}, u32[]{:S(2)}, u32[]{:S(2)}) collective-permute-start(f32[192,256]{1,0:T(8,128)S(1)} %get-tuple-element.23), channel_id=1, source_target_pairs={{0,2},{1,4},{2,6},{3,0},{4,3},{5,5},{6,7},{7,1},{8,10},{9,12},{10,... | collective-permute-start | bytes 589832 | tf_op jit(solution)/shard_map/ppermute | solution.py:167
  64.1 4.7 %collective-permute-start.20 = (f32[192,256]{1,0:T(8,128)S(1)}, f32[192,256]{1,0:T(8,128)S(1)}, u32[]{:S(2)}, u32[]{:S(2)}) collective-permute-start(f32[192,256]{1,0:T(8,128)S(1)} %get-tuple-element.21), channel_id=1, source_target_pairs={{0,6},{1,0},{2,2},{3,4},{4,7},{5,1},{6,3},{7,5},{8,14},{9,8},{10,1... | collective-permute-start | bytes 589832 | tf_op jit(solution)/shard_map/ppermute | solution.py:167
  68.9 4.4 %collective-permute-done.19 = f32[192,256]{1,0:T(8,128)S(1)} collective-permute-done((f32[192,256]{1,0:T(8,128)S(1)}, f32[192,256]{1,0:T(8,128)S(1)}, u32[]{:S(2)}, u32[]{:S(2)}) %collective-permute-start.19) | collective-permute-done | bytes 196640 | tf_op jit(solution)/shard_map/ppermute | solution.py:167
  76.0 13.6 %all-gather.3.cloned.1.call-done = f32[3072,256]{1,0:T(8,128)} async-done(((f32[768,256]{1,0:T(8,128)}), f32[3072,256]{1,0:T(8,128)}) %all-gather.3.cloned.1.call-update) | async-done | bytes 3145744 | tf_op jit(solution)/shard_map/all_gather | solution.py:174
  91.8 41.1 %shard_map.119 = f32[6144,256]{1,0:T(8,128)S(1)} custom-call(s32[48]{0:T(128)S(1)} %dynamic_slice.139.row_flags, s32[24]{0:T(128)S(1)} %dynamic_slice.140.col_flags, f32[6144,3072]{1,0:T(8,128)} %inverse.3, f32[3072,256]{1,0:T(8,128)S(1)} %bitcast.46), custom_call_target="tpu_custom_call" | custom-call | flops 14495514624 | bytes 37748736 | tf_op jit(solution)/shard_map/pallas_call | solution.py:122
  132.9 2.7 copy-done.2
  139.2 15.7 %shard_map.120 = f32[6144,256]{1,0:T(8,128)S(1)} custom-call(s32[48]{0:T(128)S(1)} %dynamic_slice.162.row_flags, s32[24]{0:T(128)S(1)} %dynamic_slice.163.col_flags, f32[6144,3072]{1,0:T(8,128)} %inverse.3, f32[3072,256]{1,0:T(8,128)S(1)} %bitcast.47), custom_call_target="tpu_custom_call" | custom-call | flops 14495514624 | bytes 37748736 | tf_op jit(solution)/shard_map/pallas_call | solution.py:122
  155.0 2.7 copy-done.1
  162.5 5.4 %collective-permute-start.8 = (f32[768,256]{1,0:T(8,128)S(1)}, f32[768,256]{1,0:T(8,128)S(1)}, u32[]{:S(2)}, u32[]{:S(2)}) collective-permute-start(f32[768,256]{1,0:T(8,128)S(1)} %dynamic-slice_add_fusion.1), channel_id=1, source_target_pairs={{0,2},{1,7},{2,4},{3,1},{4,6},{5,3},{6,0},{7,5},{8,10},{9,15},{10,... | collective-permute-start | bytes 2359304 | tf_op jit(solution)/shard_map/ppermute | solution.py:201
  167.9 3.6 %collective-permute-start.11 = (f32[768,256]{1,0:T(8,128)}, f32[768,256]{1,0:T(8,128)S(1)}, u32[]{:S(2)}, u32[]{:S(2)}) collective-permute-start(f32[768,256]{1,0:T(8,128)} %get-tuple-element.14), channel_id=1, source_target_pairs={{0,1},{1,0},{2,3},{3,2},{4,5},{5,4},{6,7},{7,6},{8,9},{9,8},{10,11... | collective-permute-start | bytes 2359304 | tf_op jit(solution)/shard_map/ppermute | solution.py:194
  172.8 16.9 %collective-permute-done.8 = f32[768,256]{1,0:T(8,128)S(1)} collective-permute-done((f32[768,256]{1,0:T(8,128)S(1)}, f32[768,256]{1,0:T(8,128)S(1)}, u32[]{:S(2)}, u32[]{:S(2)}) %collective-permute-start.8) | collective-permute-done | bytes 786464 | tf_op jit(solution)/shard_map/ppermute | solution.py:201
  191.3 2.9 collective-permute-start.13
  194.4 12.1 %collective-permute-done.22 = f32[768,256]{1,0:T(8,128)S(1)} collective-permute-done((f32[768,256]{1,0:T(8,128)S(1)}, f32[768,256]{1,0:T(8,128)S(1)}, u32[]{:S(2)}, u32[]{:S(2)}) %collective-permute-start.22) | collective-permute-done | bytes 786464 | tf_op jit(solution)/shard_map/ppermute | solution.py:201
  206.5 2.2 add_add_fusion.1
  208.7 14.7 %collective-permute-done.10 = f32[768,256]{1,0:T(8,128)S(1)} collective-permute-done((f32[768,256]{1,0:T(8,128)S(1)}, f32[768,256]{1,0:T(8,128)S(1)}, u32[]{:S(2)}, u32[]{:S(2)}) %collective-permute-start.10) | collective-permute-done | bytes 786464 | tf_op jit(solution)/shard_map/ppermute | solution.py:201
  223.4 2.2 add_add_fusion.2
  226.3 2.9 collective-permute-start.27
  229.2 11.2 %collective-permute-done.24 = f32[768,256]{1,0:T(8,128)} collective-permute-done((f32[768,256]{1,0:T(8,128)}, f32[768,256]{1,0:T(8,128)}, u32[]{:S(2)}, u32[]{:S(2)}) %collective-permute-start.24) | collective-permute-done | bytes 786464 | tf_op jit(solution)/shard_map/ppermute | solution.py:201
  240.3 2.7 add_add_fusion
  244.7 12.5 %collective-permute-done.12 = f32[768,256]{1,0:T(8,128)} collective-permute-done((f32[768,256]{1,0:T(8,128)}, f32[768,256]{1,0:T(8,128)}, u32[]{:S(2)}, u32[]{:S(2)}) %collective-permute-start.12) | collective-permute-done | bytes 786464 | tf_op jit(solution)/shard_map/ppermute | solution.py:201
  260.9 13.0 %collective-permute-done.26 = f32[768,256]{1,0:T(8,128)} collective-permute-done((f32[768,256]{1,0:T(8,128)}, f32[768,256]{1,0:T(8,128)}, u32[]{:S(2)}, u32[]{:S(2)}) %collective-permute-start.26) | collective-permute-done | bytes 786464 | tf_op jit(solution)/shard_map/ppermute | solution.py:201
  273.8 2.4 convolution_bitcast_fusion.1
  277.2 35.4 %shard_map.121 = f32[4,8,24,256]{3,2,1,0:T(8,128)} custom-call(f32[4,8,24,256]{3,2,1,0:T(8,128)} %bitcast.50), custom_call_target="tpu_custom_call" | custom-call | tf_op jit(solution)/shard_map/pallas_call | solution.py:278
  317.5 2.8 fusion.1
  (103 shorter events, 42.1 us)
Async XLA Ops:
  7.2 306.5 %copy-start = (f32[256,256]{1,0:T(8,128)S(1)}, f32[256,256]{1,0:T(8,128)}, u32[]{:S(2)}) copy-start(f32[256,256]{1,0:T(8,128)} %param.11) | copy-start | bytes 786436
  7.2 82.4 %all-gather.3.cloned.1.call-start = ((), (), s32[]{:S(2)}) async-start(), calls=%async_computation | async-start | bytes 3932160 | tf_op jit(solution)/shard_map/all_gather | solution.py:174
  8.6 9.3 %collective-permute-start.2 = (f32[192,256]{1,0:T(8,128)S(1)}, f32[192,256]{1,0:T(8,128)S(1)}, u32[]{:S(2)}, u32[]{:S(2)}) collective-permute-start(f32[192,256]{1,0:T(8,128)S(1)} %get-tuple-element.40), channel_id=1, source_target_pairs={{0,24},{8,0},{16,8},{24,16},{1,25},{9,1},{17,9},{25,17},{2,26},{10... | collective-permute-start | bytes 589832 | tf_op jit(solution)/shard_map/ppermute | solution.py:161
  12.6 10.6 %collective-permute-start.1 = (f32[192,256]{1,0:T(8,128)S(1)}, f32[192,256]{1,0:T(8,128)S(1)}, u32[]{:S(2)}, u32[]{:S(2)}) collective-permute-start(f32[192,256]{1,0:T(8,128)S(1)} %get-tuple-element.38), channel_id=1, source_target_pairs={{0,16},{8,24},{16,0},{24,8},{1,17},{9,25},{17,1},{25,9},{2,18},{10... | collective-permute-start | bytes 589832 | tf_op jit(solution)/shard_map/ppermute | solution.py:161
  13.1 10.1 %collective-permute-start = (f32[192,256]{1,0:T(8,128)S(1)}, f32[192,256]{1,0:T(8,128)S(1)}, u32[]{:S(2)}, u32[]{:S(2)}) collective-permute-start(f32[192,256]{1,0:T(8,128)S(1)} %get-tuple-element.39), channel_id=1, source_target_pairs={{0,8},{8,16},{16,24},{24,0},{1,9},{9,17},{17,25},{25,1},{2,10},{10... | collective-permute-start | bytes 589832 | tf_op jit(solution)/shard_map/ppermute | solution.py:161
  23.3 12.0 %collective-permute-start.3 = (f32[192,256]{1,0:T(8,128)S(1)}, f32[192,256]{1,0:T(8,128)S(1)}, u32[]{:S(2)}, u32[]{:S(2)}) collective-permute-start(f32[192,256]{1,0:T(8,128)S(1)} %get-tuple-element.36), channel_id=1, source_target_pairs={{0,0},{1,2},{2,4},{3,6},{4,1},{5,3},{6,5},{7,7},{8,8},{9,10},{10,1... | collective-permute-start | bytes 589832 | tf_op jit(solution)/shard_map/ppermute | solution.py:167
  24.0 15.7 %collective-permute-start.4 = (f32[192,256]{1,0:T(8,128)S(1)}, f32[192,256]{1,0:T(8,128)S(1)}, u32[]{:S(2)}, u32[]{:S(2)}) collective-permute-start(f32[192,256]{1,0:T(8,128)S(1)} %get-tuple-element.35), channel_id=1, source_target_pairs={{0,2},{1,4},{2,6},{3,0},{4,3},{5,5},{6,7},{7,1},{8,10},{9,12},{10,... | collective-permute-start | bytes 589832 | tf_op jit(solution)/shard_map/ppermute | solution.py:167
  30.4 10.5 %collective-permute-start.5 = (f32[192,256]{1,0:T(8,128)S(1)}, f32[192,256]{1,0:T(8,128)S(1)}, u32[]{:S(2)}, u32[]{:S(2)}) collective-permute-start(f32[192,256]{1,0:T(8,128)S(1)} %get-tuple-element.34), channel_id=1, source_target_pairs={{0,4},{1,6},{2,0},{3,2},{4,5},{5,7},{6,1},{7,3},{8,12},{9,14},{10,... | collective-permute-start | bytes 589832 | tf_op jit(solution)/shard_map/ppermute | solution.py:167
  32.6 8.3 %collective-permute-start.6 = (f32[192,256]{1,0:T(8,128)S(1)}, f32[192,256]{1,0:T(8,128)S(1)}, u32[]{:S(2)}, u32[]{:S(2)}) collective-permute-start(f32[192,256]{1,0:T(8,128)S(1)} %get-tuple-element.33), channel_id=1, source_target_pairs={{0,6},{1,0},{2,2},{3,4},{4,7},{5,1},{6,3},{7,5},{8,14},{9,8},{10,1... | collective-permute-start | bytes 589832 | tf_op jit(solution)/shard_map/ppermute | solution.py:167
  42.0 95.0 %all-gather.5.cloned.1.call-start = ((), (), s32[]{:S(2)}) async-start(), calls=%async_computation.1 | async-start | bytes 3932160 | tf_op jit(solution)/shard_map/all_gather | solution.py:174
  42.2 5.7 %collective-permute-start.16 = (f32[192,256]{1,0:T(8,128)S(1)}, f32[192,256]{1,0:T(8,128)S(1)}, u32[]{:S(2)}, u32[]{:S(2)}) collective-permute-start(f32[192,256]{1,0:T(8,128)S(1)} %get-tuple-element.26), channel_id=1, source_target_pairs={{0,24},{8,0},{16,8},{24,16},{1,25},{9,1},{17,9},{25,17},{2,26},{10... | collective-permute-start | bytes 589832 | tf_op jit(solution)/shard_map/ppermute | solution.py:161
  42.9 6.7 %collective-permute-start.15 = (f32[192,256]{1,0:T(8,128)S(1)}, f32[192,256]{1,0:T(8,128)S(1)}, u32[]{:S(2)}, u32[]{:S(2)}) collective-permute-start(f32[192,256]{1,0:T(8,128)S(1)} %get-tuple-element.27), channel_id=1, source_target_pairs={{0,16},{8,24},{16,0},{24,8},{1,17},{9,25},{17,1},{25,9},{2,18},{10... | collective-permute-start | bytes 589832 | tf_op jit(solution)/shard_map/ppermute | solution.py:161
  44.0 7.7 %collective-permute-start.14 = (f32[192,256]{1,0:T(8,128)S(1)}, f32[192,256]{1,0:T(8,128)S(1)}, u32[]{:S(2)}, u32[]{:S(2)}) collective-permute-start(f32[192,256]{1,0:T(8,128)S(1)} %get-tuple-element.28), channel_id=1, source_target_pairs={{0,8},{8,16},{16,24},{24,0},{1,9},{9,17},{17,25},{25,1},{2,10},{10... | collective-permute-start | bytes 589832 | tf_op jit(solution)/shard_map/ppermute | solution.py:161
  51.9 17.0 %collective-permute-start.17 = (f32[192,256]{1,0:T(8,128)S(1)}, f32[192,256]{1,0:T(8,128)S(1)}, u32[]{:S(2)}, u32[]{:S(2)}) collective-permute-start(f32[192,256]{1,0:T(8,128)S(1)} %get-tuple-element.24), channel_id=1, source_target_pairs={{0,0},{1,2},{2,4},{3,6},{4,1},{5,3},{6,5},{7,7},{8,8},{9,10},{10,1... | collective-permute-start | bytes 589832 | tf_op jit(solution)/shard_map/ppermute | solution.py:167
  52.6 16.3 %collective-permute-start.18 = (f32[192,256]{1,0:T(8,128)S(1)}, f32[192,256]{1,0:T(8,128)S(1)}, u32[]{:S(2)}, u32[]{:S(2)}) collective-permute-start(f32[192,256]{1,0:T(8,128)S(1)} %get-tuple-element.23), channel_id=1, source_target_pairs={{0,2},{1,4},{2,6},{3,0},{4,3},{5,5},{6,7},{7,1},{8,10},{9,12},{10,... | collective-permute-start | bytes 589832 | tf_op jit(solution)/shard_map/ppermute | solution.py:167
  63.3 9.9 %collective-permute-start.19 = (f32[192,256]{1,0:T(8,128)S(1)}, f32[192,256]{1,0:T(8,128)S(1)}, u32[]{:S(2)}, u32[]{:S(2)}) collective-permute-start(f32[192,256]{1,0:T(8,128)S(1)} %get-tuple-element.22), channel_id=1, source_target_pairs={{0,4},{1,6},{2,0},{3,2},{4,5},{5,7},{6,1},{7,3},{8,12},{9,14},{10,... | collective-permute-start | bytes 589832 | tf_op jit(solution)/shard_map/ppermute | solution.py:167
  64.1 10.4 %collective-permute-start.20 = (f32[192,256]{1,0:T(8,128)S(1)}, f32[192,256]{1,0:T(8,128)S(1)}, u32[]{:S(2)}, u32[]{:S(2)}) collective-permute-start(f32[192,256]{1,0:T(8,128)S(1)} %get-tuple-element.21), channel_id=1, source_target_pairs={{0,6},{1,0},{2,2},{3,4},{4,7},{5,1},{6,3},{7,5},{8,14},{9,8},{10,1... | collective-permute-start | bytes 589832 | tf_op jit(solution)/shard_map/ppermute | solution.py:167
  137.1 24.2 %collective-permute-start.7 = (f32[768,256]{1,0:T(8,128)S(1)}, f32[768,256]{1,0:T(8,128)S(1)}, u32[]{:S(2)}, u32[]{:S(2)}) collective-permute-start(f32[768,256]{1,0:T(8,128)S(1)} %get-tuple-element.16), channel_id=1, source_target_pairs={{0,1},{1,0},{2,3},{3,2},{4,5},{5,4},{6,7},{7,6},{8,9},{9,8},{10,11... | collective-permute-start | bytes 2359304 | tf_op jit(solution)/shard_map/ppermute | solution.py:194
  159.3 12.2 %collective-permute-start.21 = (f32[768,256]{1,0:T(8,128)}, f32[768,256]{1,0:T(8,128)S(1)}, u32[]{:S(2)}, u32[]{:S(2)}) collective-permute-start(f32[768,256]{1,0:T(8,128)} %get-tuple-element.12), channel_id=1, source_target_pairs={{0,1},{1,0},{2,3},{3,2},{4,5},{5,4},{6,7},{7,6},{8,9},{9,8},{10,11... | collective-permute-start | bytes 2359304 | tf_op jit(solution)/shard_map/ppermute | solution.py:194
  161.3 11.5 %collective-permute-start.9 = (f32[768,256]{1,0:T(8,128)}, f32[768,256]{1,0:T(8,128)}, u32[]{:S(2)}, u32[]{:S(2)}) collective-permute-start(f32[768,256]{1,0:T(8,128)} %get-tuple-element.15), channel_id=1, source_target_pairs={{0,1},{1,0},{2,3},{3,2},{4,5},{5,4},{6,7},{7,6},{8,9},{9,8},{10,11... | collective-permute-start | bytes 2359304 | tf_op jit(solution)/shard_map/ppermute | solution.py:194
  162.5 27.2 %collective-permute-start.8 = (f32[768,256]{1,0:T(8,128)S(1)}, f32[768,256]{1,0:T(8,128)S(1)}, u32[]{:S(2)}, u32[]{:S(2)}) collective-permute-start(f32[768,256]{1,0:T(8,128)S(1)} %dynamic-slice_add_fusion.1), channel_id=1, source_target_pairs={{0,2},{1,7},{2,4},{3,1},{4,6},{5,3},{6,0},{7,5},{8,10},{9,15},{10,... | collective-permute-start | bytes 2359304 | tf_op jit(solution)/shard_map/ppermute | solution.py:201
  167.9 40.8 %collective-permute-start.11 = (f32[768,256]{1,0:T(8,128)}, f32[768,256]{1,0:T(8,128)S(1)}, u32[]{:S(2)}, u32[]{:S(2)}) collective-permute-start(f32[768,256]{1,0:T(8,128)} %get-tuple-element.14), channel_id=1, source_target_pairs={{0,1},{1,0},{2,3},{3,2},{4,5},{5,4},{6,7},{7,6},{8,9},{9,8},{10,11... | collective-permute-start | bytes 2359304 | tf_op jit(solution)/shard_map/ppermute | solution.py:194
  171.5 22.8 %collective-permute-start.23 = (f32[768,256]{1,0:T(8,128)}, f32[768,256]{1,0:T(8,128)S(1)}, u32[]{:S(2)}, u32[]{:S(2)}) collective-permute-start(f32[768,256]{1,0:T(8,128)} %get-tuple-element.11), channel_id=1, source_target_pairs={{0,1},{1,0},{2,3},{3,2},{4,5},{5,4},{6,7},{7,6},{8,9},{9,8},{10,11... | collective-permute-start | bytes 2359304 | tf_op jit(solution)/shard_map/ppermute | solution.py:194
  172.7 33.8 %collective-permute-start.22 = (f32[768,256]{1,0:T(8,128)S(1)}, f32[768,256]{1,0:T(8,128)S(1)}, u32[]{:S(2)}, u32[]{:S(2)}) collective-permute-start(f32[768,256]{1,0:T(8,128)S(1)} %dynamic-slice_add_fusion), channel_id=1, source_target_pairs={{0,2},{1,7},{2,4},{3,1},{4,6},{5,3},{6,0},{7,5},{8,10},{9,15},{10,... | collective-permute-start | bytes 2359304 | tf_op jit(solution)/shard_map/ppermute | solution.py:201
  191.2 32.2 %collective-permute-start.10 = (f32[768,256]{1,0:T(8,128)S(1)}, f32[768,256]{1,0:T(8,128)S(1)}, u32[]{:S(2)}, u32[]{:S(2)}) collective-permute-start(f32[768,256]{1,0:T(8,128)S(1)} %add_add_fusion.3), channel_id=1, source_target_pairs={{0,2},{1,7},{2,4},{3,1},{4,6},{5,3},{6,0},{7,5},{8,10},{9,15},{10,... | collective-permute-start | bytes 2359304 | tf_op jit(solution)/shard_map/ppermute | solution.py:201
  191.3 52.5 %collective-permute-start.13 = (f32[768,256]{1,0:T(8,128)}, f32[768,256]{1,0:T(8,128)S(1)}, u32[]{:S(2)}, u32[]{:S(2)}) collective-permute-start(f32[768,256]{1,0:T(8,128)} %get-tuple-element.13), channel_id=1, source_target_pairs={{0,1},{1,0},{2,3},{3,2},{4,5},{5,4},{6,7},{7,6},{8,9},{9,8},{10,11... | collective-permute-start | bytes 2359304 | tf_op jit(solution)/shard_map/ppermute | solution.py:194
  194.3 64.7 %copy-start.5 = (f32[768,256]{1,0:T(8,128)S(1)}, f32[768,256]{1,0:T(8,128)}, u32[]{:S(2)}) copy-start(f32[768,256]{1,0:T(8,128)} %param.9) | copy-start | bytes 2359300
  194.3 34.9 %collective-permute-start.25 = (f32[768,256]{1,0:T(8,128)}, f32[768,256]{1,0:T(8,128)}, u32[]{:S(2)}, u32[]{:S(2)}) collective-permute-start(f32[768,256]{1,0:T(8,128)} %get-tuple-element.10), channel_id=1, source_target_pairs={{0,1},{1,0},{2,3},{3,2},{4,5},{5,4},{6,7},{7,6},{8,9},{9,8},{10,11... | collective-permute-start | bytes 2359304 | tf_op jit(solution)/shard_map/ppermute | solution.py:194
  208.7 31.6 %collective-permute-start.24 = (f32[768,256]{1,0:T(8,128)}, f32[768,256]{1,0:T(8,128)}, u32[]{:S(2)}, u32[]{:S(2)}) collective-permute-start(f32[768,256]{1,0:T(8,128)} %add_add_fusion.1), channel_id=1, source_target_pairs={{0,2},{1,7},{2,4},{3,1},{4,6},{5,3},{6,0},{7,5},{8,10},{9,15},{10,... | collective-permute-start | bytes 2359304 | tf_op jit(solution)/shard_map/ppermute | solution.py:201
  225.5 31.6 %collective-permute-start.12 = (f32[768,256]{1,0:T(8,128)}, f32[768,256]{1,0:T(8,128)}, u32[]{:S(2)}, u32[]{:S(2)}) collective-permute-start(f32[768,256]{1,0:T(8,128)} %add_add_fusion.2), channel_id=1, source_target_pairs={{0,2},{1,7},{2,4},{3,1},{4,6},{5,3},{6,0},{7,5},{8,10},{9,15},{10,... | collective-permute-start | bytes 2359304 | tf_op jit(solution)/shard_map/ppermute | solution.py:201
  226.3 34.6 %collective-permute-start.27 = (f32[768,256]{1,0:T(8,128)}, f32[768,256]{1,0:T(8,128)S(1)}, u32[]{:S(2)}, u32[]{:S(2)}) collective-permute-start(f32[768,256]{1,0:T(8,128)} %get-tuple-element.9), channel_id=1, source_target_pairs={{0,1},{1,0},{2,3},{3,2},{4,5},{5,4},{6,7},{7,6},{8,9},{9,8},{10,11... | collective-permute-start | bytes 2359304 | tf_op jit(solution)/shard_map/ppermute | solution.py:194
  243.0 30.9 %collective-permute-start.26 = (f32[768,256]{1,0:T(8,128)}, f32[768,256]{1,0:T(8,128)}, u32[]{:S(2)}, u32[]{:S(2)}) collective-permute-start(f32[768,256]{1,0:T(8,128)} %add_add_fusion), channel_id=1, source_target_pairs={{0,2},{1,7},{2,4},{3,1},{4,6},{5,3},{6,0},{7,5},{8,10},{9,15},{10,... | collective-permute-start | bytes 2359304 | tf_op jit(solution)/shard_map/ppermute | solution.py:201
  (10 other events, 236.1 us)
Sparse Core Ops, SparseCore 0:
  42.1 47.3 all-gather.2
  91.4 43.8 all-gather.4
